TPU v7x, 256 devices: a whole 4x4x8 slice. The times are simulated.
256 devices in a mesh: feat: 128 (over y, x, z), samp: 2 (over core).
Axes of the slice: x: 4, y: 4, z: 8, core: 2. Of those that a mesh axis runs over, the one named last changes fastest.
Arguments:
- spectra: bfloat16 [131072, 512], P('feat', 'samp'), may hold values from -6 to 6
- pair_blocks: int32 [4096, 2], P('feat'), may hold values from -1 to 511, as said below
- windows: int32 [512, 2], replicated, may hold values from 0 to 20918, as said below
Outputs:
- corr: float32 [4096, 256, 256], P(('feat', 'samp'))
- profiles: bfloat16 [131072, 512], P('feat', 'samp')
Inputs may be any that keep to these rules, and one draw needn't show every extreme that they name: `pair_blocks`: slots lie in groups of 8; slot s of the device at index d along feat is in group g = s // 8. A live entry (i, j) has block i among the 4 blocks of device d and block j among those of device d + g, with i <= j in group 0; no pair appears twice; unused slots hold -1 in both columns. At most 8 slots of a group are live, and some group has all 8 live. `windows`: column 0 is a block's first retention index and column 1 its last, which is at least 20 larger.
All inputs are finite; a program needn't handle non-finite values.
Results may differ from a plain program's by a relative error of at most 0.0075.
Values may be sent and summed in bfloat16 or wider, within the bound.
A program may use at most 64 MiB of HBM per device.

v0:
```python
import jax
import jax.numpy as jnp
from jax import lax
from jax.sharding import PartitionSpec as P

BS = 256
BLK_DEV = 4
CAP = 8
REACH = 3
SLOTS = 32


def from_behind(value, axis, by):
    length = lax.axis_size(axis)
    pairs = [(i, i + by) for i in range(length) if 0 <= i + by < length]
    return lax.ppermute(value, axis, pairs)


def place_tiles(rows_hot, cols_hot, tiles):
    placed = jnp.einsum(
        "pa,pc,pfg->afcg", rows_hot, cols_hot, tiles, preferred_element_type=jnp.float32
    )
    count = rows_hot.shape[1] * tiles.shape[1]
    return placed.astype(jnp.bfloat16).reshape(count, count)


def body(spectra, pair_blocks, windows):
    position = lax.axis_index("feat")
    shards = lax.axis_size("samp")
    rows, width = spectra.shape
    values = spectra.astype(jnp.float32)
    sums, squares = lax.psum((jnp.sum(values, axis=1), jnp.sum(values * values, axis=1)), "samp")
    total = width * shards
    mean = sums / total
    var = squares / total - mean * mean
    inv = lax.rsqrt(var + 1e-05)
    z = ((values - mean[:, None]) * inv[:, None]).astype(jnp.bfloat16).reshape(BLK_DEV, BS, width)
    z_flat = z.reshape(rows, width)
    pieces = [z]
    for offset in range(1, REACH + 1):
        pieces.append(from_behind(z, "feat", -offset))
    window = jnp.concatenate(pieces, axis=0)
    span = window.shape[0]
    first = pair_blocks[:, 0]
    second = pair_blocks[:, 1]
    live = first >= 0
    base = position * BLK_DEV
    near = jnp.clip(first - base, 0, BLK_DEV - 1)
    far = jnp.clip(second - base, 0, span - 1)
    ia = jnp.maximum(first, 0)
    ja = jnp.maximum(second, 0)
    lo_i = windows[ia, 0]
    hi_i = windows[ia, 1]
    lo_j = windows[ja, 0]
    hi_j = windows[ja, 1]
    intersection = jnp.maximum(jnp.minimum(hi_i, hi_j) - jnp.maximum(lo_i, lo_j), 0)
    weight = (intersection + 16).astype(jnp.float32) / (hi_i - lo_i + hi_j - lo_j + 16).astype(
        jnp.float32
    )
    weight = jnp.where(live, weight, jnp.float32(0.0))
    half = SLOTS // shards
    start = lax.axis_index("samp") * half
    grams = []
    for group in range(REACH + 1):
        lower = group * CAP
        ahead_blocks = window[group * BLK_DEV : (group + 1) * BLK_DEV]
        dense = jnp.einsum("afs,cgs->acfg", z, ahead_blocks, preferred_element_type=jnp.float32)
        near_g = near[lower : lower + CAP]
        far_g = jnp.clip(far[lower : lower + CAP] - group * BLK_DEV, 0, BLK_DEV - 1)
        grams.append(dense[near_g, far_g])
    gram = jnp.concatenate(grams, axis=0)
    shares = lax.psum_scatter(gram, "samp", scatter_dimension=0, tiled=True)
    own_weight = lax.dynamic_slice_in_dim(weight, start, half)
    corr = shares * (own_weight / total)[:, None, None]
    tiles_all = lax.all_gather(corr.astype(jnp.bfloat16), "samp", axis=0, tiled=True)
    acc = values * 0.0 + z_flat.astype(jnp.float32)
    labels = jnp.arange(BLK_DEV, dtype=jnp.int32)
    for group in range(REACH + 1):
        lower = group * CAP
        tiles = tiles_all[lower : lower + CAP]
        near_g = near[lower : lower + CAP]
        far_g = far[lower : lower + CAP]
        ahead_flat = window[group * BLK_DEV : (group + 1) * BLK_DEV].reshape(rows, width)
        home = (near_g[:, None] == labels[None, :]).astype(jnp.bfloat16)
        target = ((far_g - group * BLK_DEV)[:, None] == labels[None, :]).astype(jnp.bfloat16)
        placed = place_tiles(home, target, tiles)
        acc = acc + jnp.dot(placed, ahead_flat, preferred_element_type=jnp.float32)
        if group == 0:
            differ = (first[lower : lower + CAP] != second[lower : lower + CAP]).astype(
                jnp.bfloat16
            )
            placed_off = place_tiles(home, target * differ[:, None], tiles)
            acc = acc + jnp.dot(placed_off.T, z_flat, preferred_element_type=jnp.float32)
        else:
            outgoing = jnp.dot(placed.T, z_flat, preferred_element_type=jnp.float32)
            acc = acc + from_behind(outgoing.astype(jnp.bfloat16), "feat", group).astype(
                outgoing.dtype
            )
    profiles = acc.astype(jnp.bfloat16)
    return (corr, profiles)


def solution(mesh):
    placed = (P("feat", "samp"), P("feat", None), P())
    return jax.shard_map(
        body,
        mesh=mesh,
        in_specs=placed,
        out_specs=(P(("feat", "samp"), None, None), P("feat", "samp")),
        check_vma=False,
    )
```

profile of v0, /device:TPU:25, one launch (start us, length us, event | category | flops | bytes accessed | tf_op | source)
XLA Modules:
  0.0 265.7 jit_solution(12539413451494195936)
XLA Ops:
  7.2 0.0 reduce-scatter.2.cloned.1.call-start
  7.2 1.4 convert_reduce_fusion
  8.6 2.8 %all-reduce.4 = (f32[1024]{0:T(1024)S(1)}, f32[1024]{0:T(1024)S(1)}) all-reduce(f32[1024]{0:T(1024)S(1)} %get-tuple-element.9, f32[1024]{0:T(1024)S(1)} %get-tuple-element.8), channel_id=1, replica_groups=mesh['feat'=128,'samp'=2] {'samp'}, use_global_device_ids=true, to_apply=%region_3.0 | all-reduce | flops 2048 | bytes 16384 | tf_op jit(solution)/shard_map/psum | solution.py:32
  11.5 1.4 fusion.7
  12.8 9.9 %collective-permute-start = (bf16[4,256,256]{2,1,0:T(8,128)(2,1)S(1)}, bf16[4,256,256]{2,1,0:T(8,128)(2,1)S(1)}, u32[]{:S(2)}, u32[]{:S(2)}) collective-permute-start(bf16[4,256,256]{2,1,0:T(8,128)(2,1)S(1)} %bitcast.154), channel_id=1, source_target_pairs={{2,0},{4,2},{6,4},{8,6},{10,8},{12,10},{14,12},{16,14},{18,16},{20... | collective-permute-start | bytes 1572872 | tf_op jit(solution)/shard_map/ppermute | solution.py:16
  22.7 3.1 %collective-permute-start.1 = (bf16[4,256,256]{2,1,0:T(8,128)(2,1)S(1)}, bf16[4,256,256]{2,1,0:T(8,128)(2,1)}, u32[]{:S(2)}, u32[]{:S(2)}) collective-permute-start(bf16[4,256,256]{2,1,0:T(8,128)(2,1)S(1)} %bitcast.155), channel_id=1, source_target_pairs={{4,0},{6,2},{8,4},{10,6},{12,8},{14,10},{16,12},{18,14},{20,16},{2... | collective-permute-start | bytes 1572872 | tf_op jit(solution)/shard_map/ppermute | solution.py:16
  25.8 2.4 collective-permute-start.2
  28.2 0.8 fusion.64
  28.9 2.8 %convolution_bitcast_fusion.3 = f32[4,4,256,256]{2,3,0,1:T(8,128)} fusion(bf16[4,256,256,1]{2,1,3,0:T(8,128)(2,1)S(1)} %bitcast.158, bf16[4,256,256,1]{2,1,0,3:T(8,128)(2,1)S(1)} %bitcast.157), kind=kOutput, calls=%fused_computation.12 | convolution fusion | flops 536870912 | bytes 5242880 | tf_op jit(solution)/shard_map/afs,cgs->acfg/dot_general | solution.py:67
  31.7 0.1 fusion.46
  31.8 2.9 %gather_fusion = f32[8,256,256]{1,2,0:T(8,128)S(1)} fusion(f32[4,4,256,256]{2,3,0,1:T(8,128)} %convolution_bitcast_fusion.3, s32[8]{0:T(128)S(1)} %get-tuple-element.26), kind=kCustom, calls=%fused_computation | custom fusion | bytes 4194368 | tf_op jit(solution)/shard_map/gather | solution.py:70
  34.7 11.7 %collective-permute-done = bf16[4,256,256]{2,1,0:T(8,128)(2,1)S(1)} collective-permute-done((bf16[4,256,256]{2,1,0:T(8,128)(2,1)S(1)}, bf16[4,256,256]{2,1,0:T(8,128)(2,1)S(1)}, u32[]{:S(2)}, u32[]{:S(2)}) %collective-permute-start) | collective-permute-done | bytes 524320 | tf_op jit(solution)/shard_map/ppermute | solution.py:16
  46.3 2.8 %convolution_bitcast_fusion.2 = f32[4,4,256,256]{2,3,0,1:T(8,128)} fusion(bf16[4,256,256,1]{2,1,0,3:T(8,128)(2,1)S(1)} %bitcast.159, bf16[4,256,256]{2,1,0:T(8,128)(2,1)S(1)} %collective-permute-done), kind=kOutput, calls=%fused_computation.11 | convolution fusion | flops 536870912 | bytes 5242880 | tf_op jit(solution)/shard_map/afs,cgs->acfg/dot_general | solution.py:67
  49.1 4.2 %gather_fusion.1 = f32[8,256,256]{1,2,0:T(8,128)} fusion(f32[4,4,256,256]{2,3,0,1:T(8,128)} %convolution_bitcast_fusion.2, s32[8]{0:T(128)S(1)} %get-tuple-element.29), kind=kCustom, calls=%fused_computation.1 | custom fusion | bytes 4194368 | tf_op jit(solution)/shard_map/gather | solution.py:70
  53.3 13.7 %collective-permute-done.1 = bf16[4,256,256]{2,1,0:T(8,128)(2,1)} collective-permute-done((bf16[4,256,256]{2,1,0:T(8,128)(2,1)S(1)}, bf16[4,256,256]{2,1,0:T(8,128)(2,1)}, u32[]{:S(2)}, u32[]{:S(2)}) %collective-permute-start.1) | collective-permute-done | bytes 524320 | tf_op jit(solution)/shard_map/ppermute | solution.py:16
  67.0 3.8 %convolution_bitcast_fusion.1 = f32[4,4,256,256]{2,3,0,1:T(8,128)} fusion(bf16[4,256,256,1]{2,1,0,3:T(8,128)(2,1)S(1)} %bitcast.160, bf16[4,256,256]{2,1,0:T(8,128)(2,1)} %collective-permute-done.1), kind=kOutput, calls=%fused_computation.10 | convolution fusion | flops 536870912 | bytes 5242880 | tf_op jit(solution)/shard_map/afs,cgs->acfg/dot_general | solution.py:67
  70.8 4.2 %gather_fusion.2 = f32[8,256,256]{1,2,0:T(8,128)} fusion(f32[4,4,256,256]{2,3,0,1:T(8,128)} %convolution_bitcast_fusion.1, s32[8]{0:T(128)S(1)} %get-tuple-element.28), kind=kCustom, calls=%fused_computation.2 | custom fusion | bytes 4194368 | tf_op jit(solution)/shard_map/gather | solution.py:70
  75.0 14.9 %collective-permute-done.2 = bf16[4,256,256]{2,1,0:T(8,128)(2,1)} collective-permute-done((bf16[4,256,256]{2,1,0:T(8,128)(2,1)S(1)}, bf16[4,256,256]{2,1,0:T(8,128)(2,1)}, u32[]{:S(2)}, u32[]{:S(2)}) %collective-permute-start.2) | collective-permute-done | bytes 524320 | tf_op jit(solution)/shard_map/ppermute | solution.py:16
  89.9 3.8 %convolution_bitcast_fusion = f32[4,4,256,256]{2,3,0,1:T(8,128)} fusion(bf16[4,256,256,1]{2,1,0,3:T(8,128)(2,1)S(1)} %bitcast.161, bf16[4,256,256]{2,1,0:T(8,128)(2,1)} %collective-permute-done.2), kind=kOutput, calls=%fused_computation.9 | convolution fusion | flops 536870912 | bytes 5242880 | tf_op jit(solution)/shard_map/afs,cgs->acfg/dot_general | solution.py:67
  93.7 4.2 %gather_fusion.3 = f32[8,256,256]{1,2,0:T(8,128)} fusion(f32[4,4,256,256]{2,3,0,1:T(8,128)} %convolution_bitcast_fusion, s32[8]{0:T(128)S(1)} %get-tuple-element.27), kind=kCustom, calls=%fused_computation.3 | custom fusion | bytes 4194368 | tf_op jit(solution)/shard_map/gather | solution.py:70
  97.9 5.7 %pad_maximum_fusion = f32[32,256,256]{1,2,0:T(8,128)} fusion(f32[8,256,256]{1,2,0:T(8,128)} %gather_fusion.3, f32[8,256,256]{1,2,0:T(8,128)} %gather_fusion.2, f32[8,256,256]{1,2,0:T(8,128)} %gather_fusion.1, f32[8,256,256]{1,2,0:T(8,128)S(1)} %gather_fusion), kind=kLoop, calls=%fused_computation.8 | loop fusion | flops 6291456 | bytes 16777216 | tf_op jit(solution)/shard_map/concatenate | solution.py:71
  103.6 0.0 all-gather.2.cloned.1.call-start
  103.7 0.8 gather_fusion.4
  104.4 0.8 gather_fusion.5
  105.2 0.8 gather_fusion.6
  106.0 0.8 gather_fusion.7
  106.8 0.1 dynamic-slice_multiply_fusion
  106.8 21.5 %reduce-scatter.2.cloned.1.call-done = f32[16,256,256]{1,2,0:T(8,128)} async-done(((f32[32,256,256]{1,2,0:T(8,128)}), f32[16,256,256]{1,2,0:T(8,128)}) %reduce-scatter.2.cloned.1.call-update) | async-done | bytes 4194320 | tf_op jit(solution)/shard_map/reduce_scatter | solution.py:72
  128.3 4.8 %fusion.71 = (bf16[16,256,256]{1,2,0:T(8,128)(2,1)S(1)}, f32[16,256,256]{1,2,0:T(8,128)}) fusion(f32[16,256,256]{1,2,0:T(8,128)} %reduce-scatter.2.cloned.1.call-done, f32[16]{0:T(128)S(1)} %dynamic-slice_multiply_fusion), kind=kLoop, calls=%fused_computation.134 | loop fusion | flops 2097152 | bytes 10485824 | tf_op jit(solution)/shard_map/convert_element_type | solution.py:75
  133.2 2.4 copy.22
  135.6 0.1 add_bitcast_fusion.2
  135.8 5.3 %copy.32 = f32[16,256,256]{2,1,0:T(8,128)} copy(f32[16,256,256]{1,2,0:T(8,128)} %get-tuple-element.13) | data formatting | bytes 8388608
  141.2 15.0 %all-gather.2.cloned.1.call-done = bf16[32,256,256]{2,1,0:T(8,128)(2,1)} async-done(((bf16[16,256,256]{2,1,0:T(8,128)(2,1)}), bf16[32,256,256]{2,1,0:T(8,128)(2,1)}) %all-gather.2.cloned.1.call-update) | async-done | bytes 4194320 | tf_op jit(solution)/shard_map/all_gather | solution.py:75
  156.2 2.6 fusion.72
  158.8 1.2 convert_bitcast_fusion.4
  160.0 1.6 copy.24
  161.6 0.5 copy.46
  162.1 0.5 copy-done.2
  162.6 0.9 convolution_add_fusion.2
  163.6 1.2 convert_bitcast_fusion.3
  164.7 1.6 copy.25
  166.4 0.5 copy.47
  166.9 1.2 convert_bitcast_fusion.1
  168.0 1.6 copy.29
  169.7 0.5 copy.49
  170.2 1.4 convolution_convert_fusion.1
  171.5 1.7 fusion.73
  173.3 1.2 convert_bitcast_fusion
  174.5 1.6 copy.31
  176.1 0.5 copy.50
  176.6 1.2 convert_bitcast_fusion.2
  177.8 1.6 copy.27
  179.4 0.5 copy.48
  179.9 1.1 convolution_convert_fusion.2
  181.0 3.2 %collective-permute-start.3 = (bf16[1024,256]{1,0:T(8,128)(2,1)S(1)}, bf16[1024,256]{1,0:T(8,128)(2,1)S(1)}, u32[]{:S(2)}, u32[]{:S(2)}) collective-permute-start(bf16[1024,256]{1,0:T(8,128)(2,1)S(1)} %convolution_convert_fusion.2), channel_id=1, source_target_pairs={{0,2},{2,4},{4,6},{6,8},{8,10},{10,12},{12,14},{14,16},{16,18},{18... | collective-permute-start | bytes 1572872 | tf_op jit(solution)/shard_map/ppermute | solution.py:16
  184.2 4.2 %collective-permute-start.4 = (bf16[1024,256]{1,0:T(8,128)(2,1)S(1)}, bf16[1024,256]{1,0:T(8,128)(2,1)S(1)}, u32[]{:S(2)}, u32[]{:S(2)}) collective-permute-start(bf16[1024,256]{1,0:T(8,128)(2,1)S(1)} %convolution_convert_fusion.1), channel_id=1, source_target_pairs={{0,4},{2,6},{4,8},{6,10},{8,12},{10,14},{12,16},{14,18},{16,20},{1... | collective-permute-start | bytes 1572872 | tf_op jit(solution)/shard_map/ppermute | solution.py:16
  188.4 1.1 convolution_convert_fusion
  189.5 4.6 %collective-permute-start.5 = (bf16[1024,256]{1,0:T(8,128)(2,1)S(1)}, bf16[1024,256]{1,0:T(8,128)(2,1)S(1)}, u32[]{:S(2)}, u32[]{:S(2)}) collective-permute-start(bf16[1024,256]{1,0:T(8,128)(2,1)S(1)} %convolution_convert_fusion), channel_id=1, source_target_pairs={{0,6},{2,8},{4,10},{6,12},{8,14},{10,16},{12,18},{14,20},{16,22},{... | collective-permute-start | bytes 1572872 | tf_op jit(solution)/shard_map/ppermute | solution.py:16
  194.1 1.8 fusion.74
  195.9 1.1 convolution_add_fusion.1
  196.9 3.5 %collective-permute-done.3 = bf16[1024,256]{1,0:T(8,128)(2,1)S(1)} collective-permute-done((bf16[1024,256]{1,0:T(8,128)(2,1)S(1)}, bf16[1024,256]{1,0:T(8,128)(2,1)S(1)}, u32[]{:S(2)}, u32[]{:S(2)}) %collective-permute-start.3) | collective-permute-done | bytes 524320 | tf_op jit(solution)/shard_map/ppermute | solution.py:16
  200.4 13.9 %collective-permute-done.4 = bf16[1024,256]{1,0:T(8,128)(2,1)S(1)} collective-permute-done((bf16[1024,256]{1,0:T(8,128)(2,1)S(1)}, bf16[1024,256]{1,0:T(8,128)(2,1)S(1)}, u32[]{:S(2)}, u32[]{:S(2)}) %collective-permute-start.4) | collective-permute-done | bytes 524320 | tf_op jit(solution)/shard_map/ppermute | solution.py:16
  214.4 42.7 %collective-permute-done.5 = bf16[1024,256]{1,0:T(8,128)(2,1)S(1)} collective-permute-done((bf16[1024,256]{1,0:T(8,128)(2,1)S(1)}, bf16[1024,256]{1,0:T(8,128)(2,1)S(1)}, u32[]{:S(2)}, u32[]{:S(2)}) %collective-permute-start.5) | collective-permute-done | bytes 524320 | tf_op jit(solution)/shard_map/ppermute | solution.py:16
  257.1 1.7 fusion.5
  (21 shorter events, 0.1 us)
Async XLA Ops:
  7.2 96.5 %copy-start = (s32[512,2]{0,1:T(2,128)S(1)}, s32[512,2]{0,1:T(2,128)}, u32[]{:S(2)}) copy-start(s32[512,2]{0,1:T(2,128)} %param.5) | copy-start | bytes 12292
  7.2 121.1 %reduce-scatter.2.cloned.1.call-start = ((), (), s32[]{:S(2)}) async-start(), calls=%async_computation.1 | async-start | bytes 12582912 | tf_op jit(solution)/shard_map/reduce_scatter | solution.py:72
  12.8 33.5 %collective-permute-start = (bf16[4,256,256]{2,1,0:T(8,128)(2,1)S(1)}, bf16[4,256,256]{2,1,0:T(8,128)(2,1)S(1)}, u32[]{:S(2)}, u32[]{:S(2)}) collective-permute-start(bf16[4,256,256]{2,1,0:T(8,128)(2,1)S(1)} %bitcast.154), channel_id=1, source_target_pairs={{2,0},{4,2},{6,4},{8,6},{10,8},{12,10},{14,12},{16,14},{18,16},{20... | collective-permute-start | bytes 1572872 | tf_op jit(solution)/shard_map/ppermute | solution.py:16
  22.7 44.3 %collective-permute-start.1 = (bf16[4,256,256]{2,1,0:T(8,128)(2,1)S(1)}, bf16[4,256,256]{2,1,0:T(8,128)(2,1)}, u32[]{:S(2)}, u32[]{:S(2)}) collective-permute-start(bf16[4,256,256]{2,1,0:T(8,128)(2,1)S(1)} %bitcast.155), channel_id=1, source_target_pairs={{4,0},{6,2},{8,4},{10,6},{12,8},{14,10},{16,12},{18,14},{20,16},{2... | collective-permute-start | bytes 1572872 | tf_op jit(solution)/shard_map/ppermute | solution.py:16
  25.8 64.1 %collective-permute-start.2 = (bf16[4,256,256]{2,1,0:T(8,128)(2,1)S(1)}, bf16[4,256,256]{2,1,0:T(8,128)(2,1)}, u32[]{:S(2)}, u32[]{:S(2)}) collective-permute-start(bf16[4,256,256]{2,1,0:T(8,128)(2,1)S(1)} %bitcast.156), channel_id=1, source_target_pairs={{6,0},{8,2},{10,4},{12,6},{14,8},{16,10},{18,12},{20,14},{22,16},{... | collective-permute-start | bytes 1572872 | tf_op jit(solution)/shard_map/ppermute | solution.py:16
  103.6 3.1 %copy-start.3 = (s32[32,2]{0,1:T(2,128)S(1)}, s32[32,2]{0,1:T(2,128)}, u32[]{:S(2)}) copy-start(s32[32,2]{0,1:T(2,128)} %param.4) | copy-start | bytes 772
  103.6 52.6 %all-gather.2.cloned.1.call-start = ((), (), s32[]{:S(2)}) async-start(), calls=%async_computation.2 | async-start | bytes 6291456 | tf_op jit(solution)/shard_map/all_gather | solution.py:75
  161.6 1.0 copy-start.2
  181.0 19.4 %collective-permute-start.3 = (bf16[1024,256]{1,0:T(8,128)(2,1)S(1)}, bf16[1024,256]{1,0:T(8,128)(2,1)S(1)}, u32[]{:S(2)}, u32[]{:S(2)}) collective-permute-start(bf16[1024,256]{1,0:T(8,128)(2,1)S(1)} %convolution_convert_fusion.2), channel_id=1, source_target_pairs={{0,2},{2,4},{4,6},{6,8},{8,10},{10,12},{12,14},{14,16},{16,18},{18... | collective-permute-start | bytes 1572872 | tf_op jit(solution)/shard_map/ppermute | solution.py:16
  184.2 30.2 %collective-permute-start.4 = (bf16[1024,256]{1,0:T(8,128)(2,1)S(1)}, bf16[1024,256]{1,0:T(8,128)(2,1)S(1)}, u32[]{:S(2)}, u32[]{:S(2)}) collective-permute-start(bf16[1024,256]{1,0:T(8,128)(2,1)S(1)} %convolution_convert_fusion.1), channel_id=1, source_target_pairs={{0,4},{2,6},{4,8},{6,10},{8,12},{10,14},{12,16},{14,18},{16,20},{1... | collective-permute-start | bytes 1572872 | tf_op jit(solution)/shard_map/ppermute | solution.py:16
  189.5 67.6 %collective-permute-start.5 = (bf16[1024,256]{1,0:T(8,128)(2,1)S(1)}, bf16[1024,256]{1,0:T(8,128)(2,1)S(1)}, u32[]{:S(2)}, u32[]{:S(2)}) collective-permute-start(bf16[1024,256]{1,0:T(8,128)(2,1)S(1)} %convolution_convert_fusion), channel_id=1, source_target_pairs={{0,6},{2,8},{4,10},{6,12},{8,14},{10,16},{12,18},{14,20},{16,22},{... | collective-permute-start | bytes 1572872 | tf_op jit(solution)/shard_map/ppermute | solution.py:16
  257.1 1.7 copy-start.1
Sparse Core Ops, SparseCore 0:
  103.7 24.5 reduce-scatter.1
  135.7 20.3 all-gather.1
where the time goes:
time: 267 us; the launch traced here: 266 us
  waiting for transfers between devices  137 us (51%)
  local copies, waits for them, and re-layouts  40 us (15%)
  matrix products  29.8 us (11%)
  starting transfers between devices  27.3 us (10%)
  between operations  14.4 us (5%)
  other arithmetic  14.3 us (5%)
  blocking collectives  2.83 us (1%)
    ppermute x6, waiting for transfers between devices, from_behind(): return lax.ppermute(value, axis, pairs)  100 us
    ppermute x6, starting transfers between devices, from_behind(): return lax.ppermute(value, axis, pairs)  27.2 us
    reduce_scatter x1, waiting for transfers between devices, body(): shares = lax.psum_scatter(gram, 'samp', scatter_dimension=0, tiled=True)  21.5 us
    gather x4, local copies, waits for them, and re-layouts, body(): grams.append(dense[near_g, far_g])  15.5 us
    all_gather x1, waiting for transfers between devices, body(): lax.all_gather(corr.astype(jnp.bfloat16), 'samp', axis=0, tiled=True)  15 us
    dot_general x4, matrix products, body(): jnp.einsum('afs,cgs->acfg', z, ahead_blocks, preferred_element_type=jnp.f...  13.1 us
    unnamed x14, local copies, waits for them, and re-layouts  8.34 us
    convert_element_type x5, local copies, waits for them, and re-layouts, place_tiles(): return placed.astype(jnp.bfloat16).reshape(count, count)  8.11 us
  transfers between devices with their start and end apart: 8, of which 8 were waited for; matrix products, arithmetic and copies ran while one was open for 13% of the time, Pallas kernels for 0%

commit v1 on v0

v1 whole, which is shorter than its diff:
```python
import functools

import jax
import jax.numpy as jnp
from jax import lax
from jax.experimental import pallas as pl
from jax.experimental.pallas import tpu as pltpu
from jax.sharding import PartitionSpec as P

BS = 256
BLK_DEV = 4
CAP = 8
REACH = 3
SLOTS = 32
HOPS = REACH * BLK_DEV
SAMPLES = 512
MESH = pl.DeviceIdType.MESH
NT = (((1,), (1,)), ((), ()))


def pair_weights(pairs, windows, base, own_w, slot_w):
    lane = lax.broadcasted_iota(jnp.int32, (1, 128), 1)
    code = jnp.full((1, 128), -1, jnp.int32)
    numer = jnp.zeros((1, 128), jnp.int32)
    denom = jnp.ones((1, 128), jnp.int32)
    for p in range(SLOTS):
        i, j = pairs[0, p], pairs[1, p]
        live = i >= 0
        ia, ja = jnp.maximum(i, 0), jnp.maximum(j, 0)
        lo_i, hi_i = windows[0, ia], windows[1, ia]
        lo_j, hi_j = windows[0, ja], windows[1, ja]
        inter = jnp.maximum(jnp.minimum(hi_i, hi_j) - jnp.maximum(lo_i, lo_j), 0)
        near = i - base
        far = j - base - (p // CAP) * BLK_DEV
        here = lane == p
        code = jnp.where(here, jnp.where(live, near * BLK_DEV + far, -1), code)
        numer = jnp.where(here, jnp.where(live, inter + 16, 0), numer)
        denom = jnp.where(here, jnp.where(live, hi_i - lo_i + hi_j - lo_j + 16, 1), denom)
    weight = numer.astype(jnp.float32) / denom.astype(jnp.float32)
    row = lax.broadcasted_iota(jnp.int32, (16, 128), 0)
    wide = lax.broadcasted_iota(jnp.int32, (16, 128), 1)
    packed = jnp.zeros((16, 128), jnp.float32)
    for g in range(REACH + 1):
        hit = (row == code) & (wide // CAP == g)
        column = jnp.sum(jnp.where(hit, weight, 0.0), axis=1, keepdims=True)
        packed = jnp.where(wide // 32 == g, column, packed)
    own_w[...] = packed * (1.0 / SAMPLES)
    srow = lax.broadcasted_iota(jnp.int32, (SLOTS, 128), 0)
    swide = lax.broadcasted_iota(jnp.int32, (SLOTS, 128), 1)
    per_slot = jnp.sum(jnp.where(srow == swide, weight, 0.0), axis=1, keepdims=True)
    slot_w[...] = jnp.broadcast_to(per_slot, (SLOTS, 128))


def kernel(
    length,
    spectra, pairs, windows,
    corr, acc,
    z, ahead, behind, sib_ahead, sib_behind, sib_own, own_w, slot_w, far_w,
    send_a, recv_a, send_b, recv_b,
    send_sa, recv_sa, send_sb, recv_sb, send_so, recv_so, send_w, recv_w,
):
    me = lax.axis_index("feat")
    core = lax.axis_index("samp")
    right, left = lax.rem(me + 1, length), lax.rem(me + length - 1, length)
    to_left, to_right, to_sib = (left, core), (right, core), (me, 1 - core)

    barrier = pltpu.get_barrier_semaphore()
    for target in (to_left, to_right, to_sib):
        pl.semaphore_signal(barrier, inc=1, device_id=target, device_id_type=MESH)
    pair_weights(pairs, windows, me * BLK_DEV, own_w, slot_w)
    pl.semaphore_wait(barrier, 3)

    def remote(src, dst, send, recv, target):
        return pltpu.make_async_remote_copy(
            src_ref=src, dst_ref=dst, send_sem=send, recv_sem=recv,
            device_id=target, device_id_type=MESH,
        )

    def own_chunk(b):
        return spectra.at[pl.ds(b * BS, BS), :]

    def w_copy(h):
        source = own_w if h == 0 else far_w.at[h - 1]
        return remote(source, far_w.at[h], send_w.at[h], recv_w.at[h], to_right)

    def ahead_copy(m, source):
        return remote(source, ahead.at[m], send_a.at[m], recv_a.at[m], to_left)

    def behind_copy(m, source):
        return remote(source, behind.at[m], send_b.at[m], recv_b.at[m], to_right)

    def sib_ahead_copy(m):
        return remote(ahead.at[m], sib_ahead.at[m], send_sa.at[m], recv_sa.at[m], to_sib)

    def sib_behind_copy(m):
        return remote(behind.at[m], sib_behind.at[m], send_sb.at[m], recv_sb.at[m], to_sib)

    def sib_own_copy(b):
        return remote(own_chunk(b), sib_own.at[b], send_so.at[b], recv_so.at[b], to_sib)

    w_copy(0).start()
    for b in range(BLK_DEV):
        sib_own_copy(b).start()
        ahead_copy(b, own_chunk(b)).start()
        behind_copy(b, own_chunk(b)).start()

    def standardize(mine, other):
        x1, x2 = mine.astype(jnp.float32), other.astype(jnp.float32)
        total = jnp.sum(x1 + x2, axis=1, keepdims=True)
        squares = jnp.sum(x1 * x1 + x2 * x2, axis=1, keepdims=True)
        mean = total / SAMPLES
        var = squares / SAMPLES - mean * mean
        inv = lax.rsqrt(var + 1e-05)
        z1, z2 = (x1 - mean) * inv, (x2 - mean) * inv
        return jnp.concatenate([z1.astype(jnp.bfloat16), z2.astype(jnp.bfloat16)], axis=1)

    def gram(za, zc):
        return lax.dot_general(za, zc, NT, preferred_element_type=jnp.float32)

    def own_block(b, _):
        sib_own_copy(b).wait_recv()
        rows = pl.ds(pl.multiple_of(b * BS, BS), BS)
        zb = standardize(spectra[rows, :], sib_own[b])
        z[b] = zb
        acc[rows, :] = zb[:, :BS].astype(jnp.float32)
        return 0

    lax.fori_loop(0, BLK_DEV, own_block, 0)

    for a in range(BLK_DEV):
        tiles = []
        for c in range(BLK_DEV):
            r = min(a, c) * BLK_DEV + max(a, c)
            tiles.append((gram(z[a], z[c]) * own_w[r : r + 1, 0:1]).astype(jnp.bfloat16))
        halves = jnp.concatenate([z[c, :, :BS] for c in range(BLK_DEV)], axis=0)
        acc[a * BS : (a + 1) * BS, :] += jnp.dot(
            jnp.concatenate(tiles, axis=1), halves, preferred_element_type=jnp.float32
        )

    def slots_of_group(g, first_out):
        def one(q, _):
            p = g * CAP + q
            near = jnp.clip(pairs[0, p] - me * BLK_DEV, 0, BLK_DEV - 1)
            far = jnp.clip(pairs[1, p] - (me + g) * BLK_DEV, 0, BLK_DEV - 1)
            corr[first_out + q] = gram(z[near], z[g * BLK_DEV + far]) * slot_w[pl.ds(p, 1), 0:1]
            return 0

        lax.fori_loop(0, CAP, one, 0)

    @pl.when(core == 0)
    def _():
        slots_of_group(0, 0)

    def step(k, _):
        @pl.when(k < HOPS)
        def _():
            ahead_copy(k, ahead.at[k]).wait_recv()
            behind_copy(k, behind.at[k]).wait_recv()

            @pl.when(k < HOPS - BLK_DEV)
            def _():
                ahead_copy(k + BLK_DEV, ahead.at[k]).start()
                behind_copy(k + BLK_DEV, behind.at[k]).start()

            sib_ahead_copy(k).start()
            sib_behind_copy(k).start()
            for h in range(REACH):
                @pl.when(k == h * BLK_DEV)
                def _():
                    w_copy(h).wait_recv()
                    if h < REACH - 1:
                        w_copy(h + 1).start()

        @pl.when(k > 0)
        def _():
            m = k - 1
            g = m // BLK_DEV + 1
            c = m % BLK_DEV
            sib_ahead_copy(m).wait_recv()
            sib_behind_copy(m).wait_recv()
            za = standardize(ahead[m], sib_ahead[m])
            zb = standardize(behind[m], sib_behind[m])
            z[BLK_DEV + m] = za
            halves = jnp.concatenate([za[:, :BS], zb[:, :BS]], axis=0)
            picked = lax.broadcasted_iota(jnp.int32, (1, 128), 1) // 32 == g
            for a in range(BLK_DEV):
                wa = jnp.where(picked, own_w[pl.ds(a * BLK_DEV + c, 1), :], 0.0)
                wb = jnp.where(picked, far_w[g - 1, pl.ds(c * BLK_DEV + a, 1), :], 0.0)
                wa = jnp.max(wa, axis=1, keepdims=True)
                wb = jnp.max(wb, axis=1, keepdims=True)
                ta = (gram(z[a], za) * wa).astype(jnp.bfloat16)
                tb = (gram(z[a], zb) * wb).astype(jnp.bfloat16)
                acc[a * BS : (a + 1) * BS, :] += jnp.dot(
                    jnp.concatenate([ta, tb], axis=1), halves, preferred_element_type=jnp.float32
                )

            @pl.when((c == BLK_DEV - 1) & (core == g // 2))
            def _():
                slots_of_group(g, (g % 2) * CAP)

        return 0

    lax.fori_loop(0, HOPS + 1, step, 0)

    for h in range(REACH):
        w_copy(h).wait_send()

    def drain(m, _):
        ahead_copy(m, ahead.at[m]).wait_send()
        behind_copy(m, behind.at[m]).wait_send()
        sib_ahead_copy(m).wait_send()
        sib_behind_copy(m).wait_send()
        return 0

    lax.fori_loop(0, HOPS, drain, 0)
    for b in range(BLK_DEV):
        sib_own_copy(b).wait_send()


def body(spectra, pair_blocks, windows):
    length = lax.axis_size("feat")
    rows, width = spectra.shape
    vmem, smem = pl.BlockSpec(memory_space=pltpu.VMEM), pl.BlockSpec(memory_space=pltpu.SMEM)
    chunks = pltpu.VMEM((HOPS, BS, BS), jnp.bfloat16)
    many = pltpu.SemaphoreType.DMA((HOPS,))
    few = pltpu.SemaphoreType.DMA((BLK_DEV,))
    corr, acc = pl.pallas_call(
        functools.partial(kernel, length),
        out_shape=(
            jax.ShapeDtypeStruct((SLOTS // 2, BS, BS), jnp.float32),
            jax.ShapeDtypeStruct((rows, width), jnp.float32),
        ),
        in_specs=[vmem, smem, smem],
        out_specs=(vmem, vmem),
        scratch_shapes=[
            pltpu.VMEM((BLK_DEV + HOPS, BS, 2 * BS), jnp.bfloat16),
            chunks, chunks, chunks, chunks,
            pltpu.VMEM((BLK_DEV, BS, BS), jnp.bfloat16),
            pltpu.VMEM((16, 128), jnp.float32),
            pltpu.VMEM((SLOTS, 128), jnp.float32),
            pltpu.VMEM((REACH, 16, 128), jnp.float32),
            many, many, many, many,
            many, many, many, many,
            few, few,
            pltpu.SemaphoreType.DMA((REACH,)), pltpu.SemaphoreType.DMA((REACH,)),
        ],
        compiler_params=pltpu.CompilerParams(
            collective_id=0, has_side_effects=True, vmem_limit_bytes=40 << 20
        ),
    )(spectra, pair_blocks.T, windows.T)
    return corr * (1.0 / SAMPLES), acc.astype(jnp.bfloat16)


def solution(mesh):
    placed = (P("feat", "samp"), P("feat", None), P())
    return jax.shard_map(
        body,
        mesh=mesh,
        in_specs=placed,
        out_specs=(P(("feat", "samp"), None, None), P("feat", "samp")),
        check_vma=False,
    )
```

time: 267 us -> 60.6 us (0.23)
  the two profiles are of different devices: /device:TPU:25 before, /device:TPU:1 now
where the time goes in v1:
time: 60.6 us; the launch traced here: 60.4 us
  Pallas kernels  54.1 us (89%)
  other arithmetic  3.3 us (5%)
  local copies, waits for them, and re-layouts  2.4 us (4%)
  between operations  0.65 us (1%)
    pallas_call x1, Pallas kernels, body(): pl.pallas_call(functools.partial(kernel, length), out_shape=(jax.ShapeDty...  54.1 us
    mul x1, other arithmetic, body(): return (corr * (1.0 / SAMPLES), acc.astype(jnp.bfloat16))  2.45 us
    unnamed x6, local copies, waits for them, and re-layouts  2.4 us

profile of v1, /device:TPU:1, one launch (start us, length us, event | category | flops | bytes accessed | tf_op | source)
XLA Modules:
  0.0 60.4 jit_solution(17454123611735044404)
XLA Ops:
  0.6 0.0 copy-start
  0.6 1.0 %copy-done = bf16[1024,256]{1,0:T(8,128)(2,1)S(1)} copy-done((bf16[1024,256]{1,0:T(8,128)(2,1)S(1)}, bf16[1024,256]{1,0:T(8,128)(2,1)}, u32[]{:S(2)}) %copy-start) | copy-done | bytes 524312
  1.7 0.0 copy-start.1
  1.7 0.7 %copy-done.1 = s32[512,2]{0,1:T(2,128)S(1)} copy-done((s32[512,2]{0,1:T(2,128)S(1)}, s32[512,2]{0,1:T(2,128)}, u32[]{:S(2)}) %copy-start.1) | copy-done | bytes 4120
  2.4 0.0 copy-start.2
  2.4 0.7 %copy-done.2 = s32[32,2]{0,1:T(2,128)S(1)} copy-done((s32[32,2]{0,1:T(2,128)S(1)}, s32[32,2]{0,1:T(2,128)}, u32[]{:S(2)}) %copy-start.2) | copy-done | bytes 280
  3.0 54.1 %shard_map.50 = (f32[16,256,256]{2,1,0:T(8,128)S(1)}, f32[1024,256]{1,0:T(8,128)S(1)}) custom-call(bf16[1024,256]{1,0:T(8,128)(2,1)S(1)} %copy-done, s32[2,32]{1,0:T(2,128)S(1)} %bitcast.3, s32[2,512]{1,0:T(2,128)S(1)} %bitcast.2), custom_call_target="tpu_custom_call" | custom-call | tf_op jit(solution)/shard_map/pallas_call | solution.py:227
  57.1 2.5 %broadcast_multiply_fusion = f32[16,256,256]{2,1,0:T(8,128)} fusion(f32[16,256,256]{2,1,0:T(8,128)S(1)} %get-tuple-element.4), kind=kLoop, calls=%fused_computation | loop fusion | flops 1048576 | bytes 8388608 | tf_op jit(solution)/shard_map/mul | solution.py:251
  59.6 0.8 %convert_element_type.3 = bf16[1024,256]{1,0:T(8,128)(2,1)} convert(f32[1024,256]{1,0:T(8,128)S(1)} %get-tuple-element.5) | non-fusion elementwise | flops 262144 | bytes 1572864 | tf_op jit(solution)/shard_map/convert_element_type | solution.py:251
Async XLA Ops:
  0.6 1.0 %copy-start = (bf16[1024,256]{1,0:T(8,128)(2,1)S(1)}, bf16[1024,256]{1,0:T(8,128)(2,1)}, u32[]{:S(2)}) copy-start(bf16[1024,256]{1,0:T(8,128)(2,1)} %spectra.1) | copy-start | bytes 1572868
  1.7 0.7 %copy-start.1 = (s32[512,2]{0,1:T(2,128)S(1)}, s32[512,2]{0,1:T(2,128)}, u32[]{:S(2)}) copy-start(s32[512,2]{0,1:T(2,128)} %param.5) | copy-start | bytes 12292
  2.4 0.7 %copy-start.2 = (s32[32,2]{0,1:T(2,128)S(1)}, s32[32,2]{0,1:T(2,128)}, u32[]{:S(2)}) copy-start(s32[32,2]{0,1:T(2,128)} %param.4) | copy-start | bytes 772

commit v2 on v1

v2 whole, which is shorter than its diff:
```python
import functools

import jax
import jax.numpy as jnp
from jax import lax
from jax.experimental import pallas as pl
from jax.experimental.pallas import tpu as pltpu
from jax.sharding import PartitionSpec as P

BS = 256
BLK_DEV = 4
CAP = 8
REACH = 3
SLOTS = 32
HOPS = REACH * BLK_DEV
LAST = HOPS - 1
HALF = BS // 2
COLUMN = 8
SAMPLES = 512
MESH = pl.DeviceIdType.MESH
NT = (((1,), (1,)), ((), ()))


def pair_weights(pairs, windows, base, own_w):
    lane = lax.broadcasted_iota(jnp.int32, (1, 128), 1)
    code = jnp.full((1, 128), -1, jnp.int32)
    numer = jnp.zeros((1, 128), jnp.int32)
    denom = jnp.ones((1, 128), jnp.int32)
    for p in range(SLOTS):
        i, j = pairs[0, p], pairs[1, p]
        live = i >= 0
        ia, ja = jnp.maximum(i, 0), jnp.maximum(j, 0)
        lo_i, hi_i = windows[0, ia], windows[1, ia]
        lo_j, hi_j = windows[0, ja], windows[1, ja]
        inter = jnp.maximum(jnp.minimum(hi_i, hi_j) - jnp.maximum(lo_i, lo_j), 0)
        near = i - base
        far = j - base - (p // CAP) * BLK_DEV
        here = lane == p
        code = jnp.where(here, jnp.where(live, near * BLK_DEV + far, -1), code)
        numer = jnp.where(here, jnp.where(live, inter + 16, 0), numer)
        denom = jnp.where(here, jnp.where(live, hi_i - lo_i + hi_j - lo_j + 16, 1), denom)
    weight = numer.astype(jnp.float32) / denom.astype(jnp.float32)
    row = lax.broadcasted_iota(jnp.int32, (16, 128), 0)
    wide = lax.broadcasted_iota(jnp.int32, (16, 128), 1)
    packed = jnp.zeros((16, 128), jnp.float32)
    for g in range(REACH + 1):
        hit = (row == code) & (wide // CAP == g)
        column = jnp.sum(jnp.where(hit, weight, 0.0), axis=1, keepdims=True)
        packed = jnp.where(wide // 32 == g, column, packed)
    own_w[...] = packed * (1.0 / SAMPLES)


def kernel(
    length,
    spectra, pairs_in, windows_in,
    corr, profiles,
    own, acc, z, both, stash, ahead, behind, sib_ahead, sib_behind, sib_own, own_w, far_w, pairs, windows,
    send_a, recv_a, send_b, recv_b,
    send_sa, recv_sa, send_sb, recv_sb, send_so, recv_so, send_w, recv_w, load_sem, table_sem,
):
    me = lax.axis_index("feat")
    core = lax.axis_index("samp")
    has_left, has_right = me > 0, me < length - 1
    to_left, to_right, to_sib = (me - 1, core), (me + 1, core), (me, 1 - core)

    def has_ahead(m):
        return me + 1 + m // BLK_DEV < length

    def has_behind(m):
        return me - 1 - m // BLK_DEV >= 0

    barrier = pltpu.get_barrier_semaphore()

    def greet(target):
        pl.semaphore_signal(barrier, inc=1, device_id=target, device_id_type=MESH)

    pl.when(has_left)(lambda: greet(to_left))
    pl.when(has_right)(lambda: greet(to_right))
    greet(to_sib)

    def own_chunk(b):
        return spectra.at[pl.ds(b * BS, BS), :]

    def load(b):
        return pltpu.make_async_copy(own_chunk(b), own.at[b], load_sem.at[b])

    tables = (
        pltpu.make_async_copy(pairs_in, pairs, table_sem.at[0]),
        pltpu.make_async_copy(windows_in, windows, table_sem.at[1]),
    )
    for copy in tables:
        copy.start()
    for b in range(BLK_DEV):
        load(b).start()
    pl.when(has_left & has_right)(lambda: pl.semaphore_wait(barrier, 3))
    pl.when(jnp.logical_not(has_left & has_right))(lambda: pl.semaphore_wait(barrier, 2))

    def remote(src, dst, send, recv, target):
        return pltpu.make_async_remote_copy(
            src_ref=src, dst_ref=dst, send_sem=send, recv_sem=recv,
            device_id=target, device_id_type=MESH,
        )

    def w_copy(h):
        source = own_w if h == 0 else far_w.at[h - 1]
        return remote(source, far_w.at[h], send_w.at[h], recv_w.at[h], to_right)

    def ahead_copy(m, source):
        return remote(source, ahead.at[m], send_a.at[m], recv_a.at[m], to_left)

    def behind_copy(m, source):
        return remote(source, behind.at[m], send_b.at[m], recv_b.at[m], to_right)

    def rows_of(part):
        return pl.ds(part * HALF, HALF)

    def last_copy(part):
        source = behind.at[LAST - BLK_DEV, rows_of(part), :]
        target = behind.at[LAST, rows_of(part), :]
        return remote(source, target, send_b.at[LAST + part], recv_b.at[LAST + part], to_right)

    def sib_ahead_copy(m):
        return remote(ahead.at[m], sib_ahead.at[m], send_sa.at[m], recv_sa.at[m], to_sib)

    def sib_behind_copy(m):
        return remote(behind.at[m], sib_behind.at[m], send_sb.at[m], recv_sb.at[m], to_sib)

    def sib_last_copy(part):
        source = behind.at[LAST, rows_of(part), :]
        target = sib_behind.at[LAST, rows_of(part), :]
        return remote(source, target, send_sb.at[LAST + part], recv_sb.at[LAST + part], to_sib)

    def sib_own_copy(b):
        return remote(own_chunk(b), sib_own.at[b], send_so.at[b], recv_so.at[b], to_sib)

    for b in range(BLK_DEV):
        pl.when(has_left)(lambda b=b: ahead_copy(b, own_chunk(b)).start())
        pl.when(has_right)(lambda b=b: behind_copy(b, own_chunk(b)).start())
        sib_own_copy(b).start()
    for copy in tables:
        copy.wait()
    pair_weights(pairs, windows, me * BLK_DEV, own_w)
    pl.when(has_right)(lambda: w_copy(0).start())

    def standardize(mine, other):
        x1, x2 = mine.astype(jnp.float32), other.astype(jnp.float32)
        total = jnp.sum(x1 + x2, axis=1, keepdims=True)
        squares = jnp.sum(x1 * x1 + x2 * x2, axis=1, keepdims=True)
        mean = total / SAMPLES
        var = squares / SAMPLES - mean * mean
        inv = lax.rsqrt(var + 1e-05)
        z1, z2 = (x1 - mean) * inv, (x2 - mean) * inv
        return jnp.concatenate([z1.astype(jnp.bfloat16), z2.astype(jnp.bfloat16)], axis=1)

    def gram(za, zc):
        return lax.dot_general(za, zc, NT, preferred_element_type=jnp.float32)

    def dot(x, y):
        return jnp.dot(x, y, preferred_element_type=jnp.float32)

    def rows_at(a):
        return slice(a * BS, (a + 1) * BS)

    def own_block(b, _):
        load(b).wait()
        sib_own_copy(b).wait_recv()
        zb = standardize(own[b], sib_own[b])
        rows = pl.ds(pl.multiple_of(b * BS, BS), BS)
        z[rows, :] = zb
        acc[rows, :] = zb[:, :BS].astype(jnp.float32)
        return 0

    lax.fori_loop(0, BLK_DEV, own_block, 0)

    for a in range(BLK_DEV):
        tiles = []
        for c in range(BLK_DEV):
            r = min(a, c) * BLK_DEV + max(a, c)
            tile = gram(z[rows_at(a), :], z[rows_at(c), :]) * own_w[r : r + 1, 0:1]
            if a <= c:
                stash[a * BLK_DEV + c] = tile
            tiles.append(tile.astype(jnp.bfloat16))
        acc[rows_at(a), :] += dot(jnp.concatenate(tiles, axis=1), z[:, :BS])

    def slots_of_group(g):
        def one(q, _):
            i, j = pairs[0, g * CAP + q], pairs[1, g * CAP + q]
            near = jnp.clip(i - me * BLK_DEV, 0, BLK_DEV - 1)
            far = jnp.clip(j - (me + g) * BLK_DEV, 0, BLK_DEV - 1)
            tile = stash[near * BLK_DEV + far]
            corr[(g % 2) * CAP + q] = jnp.where(i >= 0, tile, 0.0)
            return 0

        lax.fori_loop(0, CAP, one, 0)

    @pl.when(core == 0)
    def _():
        slots_of_group(0)

    def receive_ahead(k):
        @pl.when(has_ahead(k))
        def _():
            ahead_copy(k, ahead.at[k]).wait_recv()
            sib_ahead_copy(k).start()

            @pl.when(has_left & (k < HOPS - BLK_DEV))
            def _():
                ahead_copy(k + BLK_DEV, ahead.at[k]).start()

    def receive_behind(k):
        @pl.when(has_behind(k))
        def _():
            behind_copy(k, behind.at[k]).wait_recv()
            sib_behind_copy(k).start()

            @pl.when(has_right & (k < LAST - BLK_DEV))
            def _():
                behind_copy(k + BLK_DEV, behind.at[k]).start()

            @pl.when(has_right & (k == LAST - BLK_DEV))
            def _():
                last_copy(0).start()
                last_copy(1).start()

        for h in range(REACH):
            @pl.when(has_behind(k) & (k == h * BLK_DEV))
            def _():
                w_copy(h).wait_recv()
                if h < REACH - 1:
                    pl.when(has_right)(lambda: w_copy(h + 1).start())

    def receive_last(part):
        last_copy(part).wait_recv()
        sib_last_copy(part).start()

    def weight(table, row, g, there):
        picked = (lax.broadcasted_iota(jnp.int32, (1, 128), 1) // 32 == g) & there
        return jnp.max(jnp.where(picked, table[pl.ds(row, 1), :], 0.0), axis=1, keepdims=True)

    def process(m, n):
        there_a, there_b = has_ahead(m), (n >= 0) & has_behind(n)
        n = jnp.maximum(n, 0)
        g, c = m // BLK_DEV + 1, m % BLK_DEV
        h, d = n // BLK_DEV + 1, n % BLK_DEV

        @pl.when(there_a)
        def _():
            sib_ahead_copy(m).wait_recv()
            both[:BS, :] = standardize(ahead[m], sib_ahead[m])

        @pl.when(jnp.logical_not(there_a))
        def _():
            both[:BS, :] = jnp.zeros((BS, 2 * BS), jnp.bfloat16)

        @pl.when(there_b)
        def _():
            sib_behind_copy(n).wait_recv()
            both[BS:, :] = standardize(behind[n], sib_behind[n])

        @pl.when(jnp.logical_not(there_b))
        def _():
            both[BS:, :] = jnp.zeros((BS, 2 * BS), jnp.bfloat16)

        grams = gram(z[...], both[...])
        tiles = []
        for a in range(BLK_DEV):
            wa = weight(own_w, a * BLK_DEV + c, g, there_a)
            wb = weight(far_w.at[h - 1], d * BLK_DEV + a, h, there_b)
            ta, tb = grams[rows_at(a), :BS] * wa, grams[rows_at(a), BS:] * wb
            stash[a * BLK_DEV + c] = ta
            tiles.append(jnp.concatenate([ta.astype(jnp.bfloat16), tb.astype(jnp.bfloat16)], axis=1))
        acc[...] += dot(jnp.concatenate(tiles, axis=0), both[:, :BS])

        @pl.when((c == BLK_DEV - 1) & (core == g // 2) & (g < REACH))
        def _():
            slots_of_group(g)

    def add_behind(m, rows):
        block = standardize(behind[m, rows, :], sib_behind[m, rows, :])
        grams = gram(z[...], block)
        tiles = []
        for a in range(BLK_DEV):
            w = weight(far_w.at[REACH - 1], m % BLK_DEV * BLK_DEV + a, REACH, True)
            tiles.append((grams[rows_at(a), :] * w).astype(jnp.bfloat16))
        acc[...] += dot(jnp.concatenate(tiles, axis=0), block[:, :BS])

    early = me % COLUMN < COLUMN // 2

    def step(k, _):
        pl.when((k < LAST) & jnp.logical_not(early))(lambda: receive_behind(k))
        pl.when(k < HOPS)(lambda: receive_ahead(k))
        pl.when((k > 0) & (k < HOPS) & early)(lambda: receive_behind(k - 1))
        pl.when((k == HOPS) & has_behind(LAST))(lambda: receive_last(0))
        pl.when(k > 0)(lambda: process(k - 1, k - 2))
        return 0

    lax.fori_loop(0, HOPS + 1, step, 0)

    @pl.when(has_behind(LAST))
    def _():
        receive_last(1)
        sib_last_copy(0).wait_recv()
        add_behind(LAST, rows_of(0))

    @pl.when(core == REACH // 2)
    def _():
        slots_of_group(REACH)

    @pl.when(has_behind(LAST))
    def _():
        sib_last_copy(1).wait_recv()
        add_behind(LAST, rows_of(1))

    for a in range(BLK_DEV):
        profiles[a] = acc[rows_at(a), :].astype(jnp.bfloat16)

    for h in range(REACH):
        sent = has_right if h == 0 else has_right & has_behind((h - 1) * BLK_DEV)
        pl.when(sent)(lambda h=h: w_copy(h).wait_send())

    def drain(m, _):
        mine = m < BLK_DEV
        sent_a = has_left & (mine | has_ahead(m - BLK_DEV))
        sent_b = has_right & (mine | has_behind(m - BLK_DEV))
        pl.when(sent_a)(lambda: ahead_copy(m, ahead.at[m]).wait_send())
        pl.when(has_ahead(m))(lambda: sib_ahead_copy(m).wait_send())
        pl.when(sent_b & (m < LAST))(lambda: behind_copy(m, behind.at[m]).wait_send())
        pl.when(has_behind(m) & (m < LAST))(lambda: sib_behind_copy(m).wait_send())
        return 0

    lax.fori_loop(0, HOPS, drain, 0)
    for part in range(2):
        sent = has_right & has_behind(LAST - BLK_DEV)
        pl.when(sent)(lambda part=part: last_copy(part).wait_send())
        pl.when(has_behind(LAST))(lambda part=part: sib_last_copy(part).wait_send())
    for b in range(BLK_DEV):
        sib_own_copy(b).wait_send()


def write_out(corr, profiles, corr_out, profiles_out, sems):
    copies = [
        pltpu.make_async_copy(corr.at[p], corr_out.at[p], sems.at[p]) for p in range(SLOTS // 2)
    ]
    copies += [
        pltpu.make_async_copy(
            profiles.at[b], profiles_out.at[pl.ds(b * BS, BS), :], sems.at[SLOTS // 2 + b]
        )
        for b in range(BLK_DEV)
    ]
    for copy in copies:
        copy.start()
    for copy in copies:
        copy.wait()


def body(spectra, pair_blocks, windows):
    length = lax.axis_size("feat")
    rows, width = spectra.shape
    vmem, hbm = pl.BlockSpec(memory_space=pltpu.VMEM), pl.BlockSpec(memory_space=pltpu.HBM)
    anywhere = pl.BlockSpec(memory_space=pl.ANY)
    chunks = pltpu.VMEM((HOPS, BS, BS), jnp.bfloat16)
    blocks = pltpu.VMEM((BLK_DEV, BS, BS), jnp.bfloat16)
    many = pltpu.SemaphoreType.DMA((HOPS,))
    more = pltpu.SemaphoreType.DMA((HOPS + 1,))
    few = pltpu.SemaphoreType.DMA((BLK_DEV,))
    corr, profiles = pl.pallas_call(
        functools.partial(kernel, length),
        out_shape=(
            jax.ShapeDtypeStruct((SLOTS // 2, BS, BS), jnp.float32),
            jax.ShapeDtypeStruct((BLK_DEV, BS, BS), jnp.bfloat16),
        ),
        in_specs=[hbm, hbm, hbm],
        out_specs=(vmem, vmem),
        scratch_shapes=[
            blocks,
            pltpu.VMEM((BLK_DEV * BS, BS), jnp.float32),
            pltpu.VMEM((BLK_DEV * BS, 2 * BS), jnp.bfloat16),
            pltpu.VMEM((2 * BS, 2 * BS), jnp.bfloat16),
            pltpu.VMEM((BLK_DEV * BLK_DEV, BS, BS), jnp.float32),
            chunks, chunks, chunks, chunks, blocks,
            pltpu.VMEM((16, 128), jnp.float32),
            pltpu.VMEM((REACH, 16, 128), jnp.float32),
            pltpu.SMEM((2, SLOTS), jnp.int32),
            pltpu.SMEM((2, windows.shape[0]), jnp.int32),
            many, many, more, more,
            many, many, more, more,
            few, few,
            pltpu.SemaphoreType.DMA((REACH,)), pltpu.SemaphoreType.DMA((REACH,)),
            few, pltpu.SemaphoreType.DMA((2,)),
        ],
        compiler_params=pltpu.CompilerParams(
            collective_id=0, has_side_effects=True, vmem_limit_bytes=40 << 20
        ),
    )(*(pltpu.with_memory_space_constraint(x, pltpu.HBM) for x in (spectra, pair_blocks.T, windows.T)))
    return pl.pallas_call(
        write_out,
        out_shape=(
            jax.ShapeDtypeStruct(corr.shape, corr.dtype),
            jax.ShapeDtypeStruct((rows, width), jnp.bfloat16),
        ),
        in_specs=[anywhere, anywhere],
        out_specs=(hbm, hbm),
        scratch_shapes=[pltpu.SemaphoreType.DMA((SLOTS // 2 + BLK_DEV,))],
        compiler_params=pltpu.CompilerParams(vmem_limit_bytes=1 << 20),
    )(corr, profiles)


def solution(mesh):
    placed = (P("feat", "samp"), P("feat", None), P())
    return jax.shard_map(
        body,
        mesh=mesh,
        in_specs=placed,
        out_specs=(P(("feat", "samp"), None, None), P("feat", "samp")),
        check_vma=False,
    )
```

time: 60.6 us -> 51.6 us (0.85)
  the two profiles are of different devices: /device:TPU:1 before, /device:TPU:25 now
where the time goes in v2:
time: 51.6 us; the launch traced here: 51.2 us
  Pallas kernels  50.5 us (98%)
  between operations  0.64 us (1%)
    pallas_call x1, Pallas kernels, body(): pl.pallas_call(functools.partial(kernel, length), out_shape=(jax.ShapeDty...  48.2 us
    pallas_call x1, Pallas kernels, body(): pl.pallas_call(write_out, out_shape=(jax.ShapeDtypeStruct(corr.shape, cor...  2.33 us

profile of v2, /device:TPU:25, one launch (start us, length us, event | category | flops | bytes accessed | tf_op | source)
XLA Modules:
  0.0 51.2 jit_solution(9462312093703108308)
XLA Ops:
  0.6 48.2 %shard_map.50 = (f32[16,256,256]{2,1,0:T(8,128)S(1)}, bf16[4,256,256]{2,1,0:T(8,128)(2,1)S(1)}) custom-call(bf16[1024,256]{1,0:T(8,128)(2,1)} %spectra.1, s32[2,32]{1,0:T(2,128)} %bitcast.3, s32[2,512]{1,0:T(2,128)} %bitcast.2), custom_call_target="tpu_custom_call" | custom-call | tf_op jit(solution)/shard_map/pallas_call | solution.py:366
  48.8 2.3 %shard_map.51 = (f32[16,256,256]{2,1,0:T(8,128)}, bf16[1024,256]{1,0:T(8,128)(2,1)}) custom-call(f32[16,256,256]{2,1,0:T(8,128)S(1)} %get-tuple-element.4.corr, bf16[4,256,256]{2,1,0:T(8,128)(2,1)S(1)} %get-tuple-element.5.profiles), custom_call_target="tpu_custom_call" | custom-call | tf_op jit(solution)/shard_map/pallas_call | solution.py:395

commit v3 on v2

--- a/solution.py
+++ b/solution.py
@@ -16,38 +16,35 @@
 LAST = HOPS - 1
 HALF = BS // 2
 COLUMN = 8
+DRAIN = 5
 SAMPLES = 512
 MESH = pl.DeviceIdType.MESH
 NT = (((1,), (1,)), ((), ()))
 
 
 def pair_weights(pairs, windows, base, own_w):
-    lane = lax.broadcasted_iota(jnp.int32, (1, 128), 1)
-    code = jnp.full((1, 128), -1, jnp.int32)
-    numer = jnp.zeros((1, 128), jnp.int32)
-    denom = jnp.ones((1, 128), jnp.int32)
-    for p in range(SLOTS):
-        i, j = pairs[0, p], pairs[1, p]
-        live = i >= 0
-        ia, ja = jnp.maximum(i, 0), jnp.maximum(j, 0)
-        lo_i, hi_i = windows[0, ia], windows[1, ia]
-        lo_j, hi_j = windows[0, ja], windows[1, ja]
-        inter = jnp.maximum(jnp.minimum(hi_i, hi_j) - jnp.maximum(lo_i, lo_j), 0)
-        near = i - base
-        far = j - base - (p // CAP) * BLK_DEV
-        here = lane == p
-        code = jnp.where(here, jnp.where(live, near * BLK_DEV + far, -1), code)
-        numer = jnp.where(here, jnp.where(live, inter + 16, 0), numer)
-        denom = jnp.where(here, jnp.where(live, hi_i - lo_i + hi_j - lo_j + 16, 1), denom)
-    weight = numer.astype(jnp.float32) / denom.astype(jnp.float32)
-    row = lax.broadcasted_iota(jnp.int32, (16, 128), 0)
-    wide = lax.broadcasted_iota(jnp.int32, (16, 128), 1)
-    packed = jnp.zeros((16, 128), jnp.float32)
+    row = lax.broadcasted_iota(jnp.int32, (CAP, 128), 0)
+    lane = lax.broadcasted_iota(jnp.int32, (CAP, 128), 1)
+    total = jnp.zeros((1, 128), jnp.float32)
     for g in range(REACH + 1):
-        hit = (row == code) & (wide // CAP == g)
-        column = jnp.sum(jnp.where(hit, weight, 0.0), axis=1, keepdims=True)
-        packed = jnp.where(wide // 32 == g, column, packed)
-    own_w[...] = packed * (1.0 / SAMPLES)
+        place = jnp.full((CAP, 128), -1, jnp.int32)
+        numer = jnp.zeros((CAP, 128), jnp.int32)
+        denom = jnp.ones((CAP, 128), jnp.int32)
+        for q in range(CAP):
+            i, j = pairs[0, g * CAP + q], pairs[1, g * CAP + q]
+            live = i >= 0
+            ia, ja = jnp.maximum(i, 0), jnp.maximum(j, 0)
+            lo_i, hi_i = windows[0, ia], windows[1, ia]
+            lo_j, hi_j = windows[0, ja], windows[1, ja]
+            inter = jnp.maximum(jnp.minimum(hi_i, hi_j) - jnp.maximum(lo_i, lo_j), 0)
+            code = (i - base) * BLK_DEV + j - base - g * BLK_DEV + g * BLK_DEV * BLK_DEV
+            here = row == q
+            place = jnp.where(here, jnp.where(live, code, -1), place)
+            numer = jnp.where(here, jnp.where(live, inter + 16, 0), numer)
+            denom = jnp.where(here, jnp.where(live, hi_i - lo_i + hi_j - lo_j + 16, 1), denom)
+        weight = numer.astype(jnp.float32) / denom.astype(jnp.float32)
+        total += jnp.sum(jnp.where(lane == place, weight, 0.0), axis=0, keepdims=True)
+    own_w[...] = total * (1.0 / SAMPLES)
 
 
 def kernel(
@@ -161,6 +158,11 @@
     def rows_at(a):
         return slice(a * BS, (a + 1) * BS)
 
+    def weight(table, g, a, c, there=True):
+        lane = lax.broadcasted_iota(jnp.int32, (1, 128), 1)
+        picked = (lane == (g * BLK_DEV + a) * BLK_DEV + c) & there
+        return jnp.max(jnp.where(picked, table[...], 0.0), axis=1, keepdims=True)
+
     def own_block(b, _):
         load(b).wait()
         sib_own_copy(b).wait_recv()
@@ -175,8 +177,8 @@
     for a in range(BLK_DEV):
         tiles = []
         for c in range(BLK_DEV):
-            r = min(a, c) * BLK_DEV + max(a, c)
-            tile = gram(z[rows_at(a), :], z[rows_at(c), :]) * own_w[r : r + 1, 0:1]
+            w = weight(own_w, 0, min(a, c), max(a, c))
+            tile = gram(z[rows_at(a), :], z[rows_at(c), :]) * w
             if a <= c:
                 stash[a * BLK_DEV + c] = tile
             tiles.append(tile.astype(jnp.bfloat16))
@@ -233,10 +235,6 @@
         last_copy(part).wait_recv()
         sib_last_copy(part).start()
 
-    def weight(table, row, g, there):
-        picked = (lax.broadcasted_iota(jnp.int32, (1, 128), 1) // 32 == g) & there
-        return jnp.max(jnp.where(picked, table[pl.ds(row, 1), :], 0.0), axis=1, keepdims=True)
-
     def process(m, n):
         there_a, there_b = has_ahead(m), (n >= 0) & has_behind(n)
         n = jnp.maximum(n, 0)
@@ -264,8 +262,8 @@
         grams = gram(z[...], both[...])
         tiles = []
         for a in range(BLK_DEV):
-            wa = weight(own_w, a * BLK_DEV + c, g, there_a)
-            wb = weight(far_w.at[h - 1], d * BLK_DEV + a, h, there_b)
+            wa = weight(own_w, g, a, c, there_a)
+            wb = weight(far_w.at[h - 1], h, d, a, there_b)
             ta, tb = grams[rows_at(a), :BS] * wa, grams[rows_at(a), BS:] * wb
             stash[a * BLK_DEV + c] = ta
             tiles.append(jnp.concatenate([ta.astype(jnp.bfloat16), tb.astype(jnp.bfloat16)], axis=1))
@@ -275,50 +273,24 @@
         def _():
             slots_of_group(g)
 
-    def add_behind(m, rows):
+    def write_profiles(total):
+        for a in range(BLK_DEV):
+            profiles[a] = total[rows_at(a), :].astype(jnp.bfloat16)
+
+    def add_behind(m, rows, final=False):
         block = standardize(behind[m, rows, :], sib_behind[m, rows, :])
         grams = gram(z[...], block)
         tiles = []
         for a in range(BLK_DEV):
-            w = weight(far_w.at[REACH - 1], m % BLK_DEV * BLK_DEV + a, REACH, True)
+            w = weight(far_w.at[REACH - 1], REACH, m % BLK_DEV, a)
             tiles.append((grams[rows_at(a), :] * w).astype(jnp.bfloat16))
-        acc[...] += dot(jnp.concatenate(tiles, axis=0), block[:, :BS])
-
-    early = me % COLUMN < COLUMN // 2
-
-    def step(k, _):
-        pl.when((k < LAST) & jnp.logical_not(early))(lambda: receive_behind(k))
-        pl.when(k < HOPS)(lambda: receive_ahead(k))
-        pl.when((k > 0) & (k < HOPS) & early)(lambda: receive_behind(k - 1))
-        pl.when((k == HOPS) & has_behind(LAST))(lambda: receive_last(0))
-        pl.when(k > 0)(lambda: process(k - 1, k - 2))
-        return 0
-
-    lax.fori_loop(0, HOPS + 1, step, 0)
-
-    @pl.when(has_behind(LAST))
-    def _():
-        receive_last(1)
-        sib_last_copy(0).wait_recv()
-        add_behind(LAST, rows_of(0))
-
-    @pl.when(core == REACH // 2)
-    def _():
-        slots_of_group(REACH)
-
-    @pl.when(has_behind(LAST))
-    def _():
-        sib_last_copy(1).wait_recv()
-        add_behind(LAST, rows_of(1))
-
-    for a in range(BLK_DEV):
-        profiles[a] = acc[rows_at(a), :].astype(jnp.bfloat16)
-
-    for h in range(REACH):
-        sent = has_right if h == 0 else has_right & has_behind((h - 1) * BLK_DEV)
-        pl.when(sent)(lambda h=h: w_copy(h).wait_send())
-
-    def drain(m, _):
+        total = acc[...] + dot(jnp.concatenate(tiles, axis=0), block[:, :BS])
+        if final:
+            write_profiles(total)
+        else:
+            acc[...] = total
+
+    def drain(m):
         mine = m < BLK_DEV
         sent_a = has_left & (mine | has_ahead(m - BLK_DEV))
         sent_b = has_right & (mine | has_behind(m - BLK_DEV))
@@ -326,15 +298,55 @@
         pl.when(has_ahead(m))(lambda: sib_ahead_copy(m).wait_send())
         pl.when(sent_b & (m < LAST))(lambda: behind_copy(m, behind.at[m]).wait_send())
         pl.when(has_behind(m) & (m < LAST))(lambda: sib_behind_copy(m).wait_send())
+
+        @pl.when(m == 0)
+        def _():
+            for b in range(BLK_DEV):
+                sib_own_copy(b).wait_send()
+
+    place = me % COLUMN
+    early, late = place < COLUMN // 2, place >= COLUMN - 2
+
+    def step(k, _):
+        pl.when((k < LAST) & late)(lambda: receive_behind(k))
+        pl.when(k < HOPS)(lambda: receive_ahead(k))
+        lag = jnp.where(early, 1, 0)
+        now = (k >= lag) & (k < LAST + lag) & jnp.logical_not(late)
+        pl.when(now)(lambda: receive_behind(k - lag))
+        pl.when((k == HOPS) & has_behind(LAST))(lambda: receive_last(0))
+        pl.when(k > 0)(lambda: process(k - 1, k - 2))
+        pl.when(k >= DRAIN)(lambda: drain(k - DRAIN))
         return 0
 
-    lax.fori_loop(0, HOPS, drain, 0)
+    lax.fori_loop(0, HOPS + 1, step, 0)
+
+    @pl.when(has_behind(LAST))
+    def _():
+        receive_last(1)
+        sib_last_copy(0).wait_recv()
+        add_behind(LAST, rows_of(0))
+
+    @pl.when(core == REACH // 2)
+    def _():
+        slots_of_group(REACH)
+
+    @pl.when(has_behind(LAST))
+    def _():
+        sib_last_copy(1).wait_recv()
+        add_behind(LAST, rows_of(1), final=True)
+
+    pl.when(jnp.logical_not(has_behind(LAST)))(lambda: write_profiles(acc[...]))
+
+    for m in range(HOPS + 1 - DRAIN, HOPS):
+        drain(m)
+    for h in range(REACH):
+        sent = has_right if h == 0 else has_right & has_behind((h - 1) * BLK_DEV)
+        pl.when(sent)(lambda h=h: w_copy(h).wait_send())
+
     for part in range(2):
         sent = has_right & has_behind(LAST - BLK_DEV)
         pl.when(sent)(lambda part=part: last_copy(part).wait_send())
         pl.when(has_behind(LAST))(lambda part=part: sib_last_copy(part).wait_send())
-    for b in range(BLK_DEV):
-        sib_own_copy(b).wait_send()
 
 
 def write_out(corr, profiles, corr_out, profiles_out, sems):
@@ -378,8 +390,8 @@
             pltpu.VMEM((2 * BS, 2 * BS), jnp.bfloat16),
             pltpu.VMEM((BLK_DEV * BLK_DEV, BS, BS), jnp.float32),
             chunks, chunks, chunks, chunks, blocks,
-            pltpu.VMEM((16, 128), jnp.float32),
-            pltpu.VMEM((REACH, 16, 128), jnp.float32),
+            pltpu.VMEM((1, 128), jnp.float32),
+            pltpu.VMEM((REACH, 1, 128), jnp.float32),
             pltpu.SMEM((2, SLOTS), jnp.int32),
             pltpu.SMEM((2, windows.shape[0]), jnp.int32),
             many, many, more, more,

time: 51.6 us -> 50.7 us (0.983)
  Pallas kernels: 50.5 us -> 49.9 us
    pallas_call x1, Pallas kernels: 48.2 us -> 47.6 us  [body(): pl.pallas_call(functools.partial(kernel, length), out_shape=(jax.ShapeDty...]
where the time goes in v3:
time: 50.7 us; the launch traced here: 50.6 us
  Pallas kernels  49.9 us (98%)
  between operations  0.64 us (1%)
    pallas_call x1, Pallas kernels, body(): pl.pallas_call(functools.partial(kernel, length), out_shape=(jax.ShapeDty...  47.6 us
    pallas_call x1, Pallas kernels, body(): pl.pallas_call(write_out, out_shape=(jax.ShapeDtypeStruct(corr.shape, cor...  2.33 us

profile of v3, /device:TPU:25, one launch (start us, length us, event | category | flops | bytes accessed | tf_op | source)
XLA Modules:
  0.0 50.6 jit_solution(4730499308200114451)
XLA Ops:
  0.6 47.6 %shard_map.50 = (f32[16,256,256]{2,1,0:T(8,128)S(1)}, bf16[4,256,256]{2,1,0:T(8,128)(2,1)S(1)}) custom-call(bf16[1024,256]{1,0:T(8,128)(2,1)} %spectra.1, s32[2,32]{1,0:T(2,128)} %bitcast.3, s32[2,512]{1,0:T(2,128)} %bitcast.2), custom_call_target="tpu_custom_call" | custom-call | tf_op jit(solution)/shard_map/pallas_call | solution.py:378
  48.2 2.3 %shard_map.51 = (f32[16,256,256]{2,1,0:T(8,128)}, bf16[1024,256]{1,0:T(8,128)(2,1)}) custom-call(f32[16,256,256]{2,1,0:T(8,128)S(1)} %get-tuple-element.4.corr, bf16[4,256,256]{2,1,0:T(8,128)(2,1)S(1)} %get-tuple-element.5.profiles), custom_call_target="tpu_custom_call" | custom-call | tf_op jit(solution)/shard_map/pallas_call | solution.py:407

commit v4 on v3

--- a/solution.py
+++ b/solution.py
@@ -51,13 +51,18 @@
     length,
     spectra, pairs_in, windows_in,
     corr, profiles,
-    own, acc, z, both, stash, ahead, behind, sib_ahead, sib_behind, sib_own, own_w, far_w, pairs, windows,
+    own, acc, z, both, stash, ahead, behind, sib_ahead, sib_behind, sib_own, tables_w, pairs, windows,
     send_a, recv_a, send_b, recv_b,
-    send_sa, recv_sa, send_sb, recv_sb, send_so, recv_so, send_w, recv_w, load_sem, table_sem,
+    send_sa, recv_sa, send_sb, recv_sb, send_so, recv_so, send_w, recv_w, load_sem, table_sem, left_in, right_in, sib_in,
 ):
     me = lax.axis_index("feat")
     core = lax.axis_index("samp")
     has_left, has_right = me > 0, me < length - 1
+
+    def greets_left(d):
+        return (d % COLUMN == 0) | (d % COLUMN == COLUMN - 1)
+
+    left_greeted, right_greets = greets_left(me), greets_left(me + 1)
     to_left, to_right, to_sib = (me - 1, core), (me + 1, core), (me, 1 - core)
 
     def has_ahead(m):
@@ -71,9 +76,12 @@
     def greet(target):
         pl.semaphore_signal(barrier, inc=1, device_id=target, device_id_type=MESH)
 
-    pl.when(has_left)(lambda: greet(to_left))
-    pl.when(has_right)(lambda: greet(to_right))
-    greet(to_sib)
+    def tell(flag, target):
+        pl.semaphore_signal(flag, inc=1, device_id=target, device_id_type=MESH)
+
+    pl.when(has_left & left_greeted)(lambda: greet(to_left))
+    pl.when(has_right & jnp.logical_not(right_greets))(lambda: greet(to_right))
+    pl.when(core == 1)(lambda: greet(to_sib))
 
     def own_chunk(b):
         return spectra.at[pl.ds(b * BS, BS), :]
@@ -89,8 +97,15 @@
         copy.start()
     for b in range(BLK_DEV):
         load(b).start()
-    pl.when(has_left & has_right)(lambda: pl.semaphore_wait(barrier, 3))
-    pl.when(jnp.logical_not(has_left & has_right))(lambda: pl.semaphore_wait(barrier, 2))
+    from_right = has_right & right_greets
+    from_left = has_left & jnp.logical_not(left_greeted)
+    one = jnp.int32(1)
+    peers = from_right * one + from_left * one + (core == 0) * one
+    for count in (1, 2, 3):
+        pl.when(peers == count)(lambda count=count: pl.semaphore_wait(barrier, count))
+    pl.when(core == 0)(lambda: tell(sib_in, to_sib))
+    pl.when(from_right)(lambda: tell(left_in, to_right))
+    pl.when(from_left)(lambda: tell(right_in, to_left))
 
     def remote(src, dst, send, recv, target):
         return pltpu.make_async_remote_copy(
@@ -99,8 +114,7 @@
         )
 
     def w_copy(h):
-        source = own_w if h == 0 else far_w.at[h - 1]
-        return remote(source, far_w.at[h], send_w.at[h], recv_w.at[h], to_right)
+        return remote(tables_w.at[h], tables_w.at[h + 1], send_w.at[h], recv_w.at[h], to_right)
 
     def ahead_copy(m, source):
         return remote(source, ahead.at[m], send_a.at[m], recv_a.at[m], to_left)
@@ -130,12 +144,33 @@
     def sib_own_copy(b):
         return remote(own_chunk(b), sib_own.at[b], send_so.at[b], recv_so.at[b], to_sib)
 
+    def send_ahead():
+        for b in range(BLK_DEV):
+            ahead_copy(b, own_chunk(b)).start()
+
+    def send_behind():
+        for b in range(BLK_DEV):
+            behind_copy(b, own_chunk(b)).start()
+
+    pl.when(from_left)(send_ahead)
+    pl.when(from_right)(send_behind)
+    pl.when(core == 1)(lambda: pl.semaphore_wait(sib_in, 1))
     for b in range(BLK_DEV):
-        pl.when(has_left)(lambda b=b: ahead_copy(b, own_chunk(b)).start())
-        pl.when(has_right)(lambda b=b: behind_copy(b, own_chunk(b)).start())
         sib_own_copy(b).start()
+
+    @pl.when(has_right & jnp.logical_not(right_greets))
+    def _():
+        pl.semaphore_wait(right_in, 1)
+        send_behind()
+
+    @pl.when(has_left & left_greeted)
+    def _():
+        pl.semaphore_wait(left_in, 1)
+        send_ahead()
+
     for copy in tables:
         copy.wait()
+    own_w = tables_w.at[0]
     pair_weights(pairs, windows, me * BLK_DEV, own_w)
     pl.when(has_right)(lambda: w_copy(0).start())
 
@@ -237,6 +272,7 @@
 
     def process(m, n):
         there_a, there_b = has_ahead(m), (n >= 0) & has_behind(n)
+        table = jnp.where(n >= 0, n // BLK_DEV + 1, 0)
         n = jnp.maximum(n, 0)
         g, c = m // BLK_DEV + 1, m % BLK_DEV
         h, d = n // BLK_DEV + 1, n % BLK_DEV
@@ -263,7 +299,7 @@
         tiles = []
         for a in range(BLK_DEV):
             wa = weight(own_w, g, a, c, there_a)
-            wb = weight(far_w.at[h - 1], h, d, a, there_b)
+            wb = weight(tables_w.at[table], h, d, a, there_b)
             ta, tb = grams[rows_at(a), :BS] * wa, grams[rows_at(a), BS:] * wb
             stash[a * BLK_DEV + c] = ta
             tiles.append(jnp.concatenate([ta.astype(jnp.bfloat16), tb.astype(jnp.bfloat16)], axis=1))
@@ -282,7 +318,7 @@
         grams = gram(z[...], block)
         tiles = []
         for a in range(BLK_DEV):
-            w = weight(far_w.at[REACH - 1], REACH, m % BLK_DEV, a)
+            w = weight(tables_w.at[REACH], REACH, m % BLK_DEV, a)
             tiles.append((grams[rows_at(a), :] * w).astype(jnp.bfloat16))
         total = acc[...] + dot(jnp.concatenate(tiles, axis=0), block[:, :BS])
         if final:
@@ -306,21 +342,47 @@
 
     place = me % COLUMN
     early, late = place < COLUMN // 2, place >= COLUMN - 2
+    lead = jnp.where(place < 2, 1, 0)
 
     def step(k, _):
         pl.when((k < LAST) & late)(lambda: receive_behind(k))
-        pl.when(k < HOPS)(lambda: receive_ahead(k))
+
+        @pl.when((k == LAST) & late & has_behind(LAST))
+        def _():
+            receive_last(0)
+            receive_last(1)
+
+        held = late & (k == LAST)
+        pl.when((k + lead < HOPS) & jnp.logical_not(held))(lambda: receive_ahead(k + lead))
         lag = jnp.where(early, 1, 0)
         now = (k >= lag) & (k < LAST + lag) & jnp.logical_not(late)
         pl.when(now)(lambda: receive_behind(k - lag))
-        pl.when((k == HOPS) & has_behind(LAST))(lambda: receive_last(0))
-        pl.when(k > 0)(lambda: process(k - 1, k - 2))
+        last_turn = (k == HOPS) & has_behind(LAST)
+        pl.when(last_turn & jnp.logical_not(late))(lambda: receive_last(0))
+
+        @pl.when(last_turn & (lead == 1))
+        def _():
+            sib_behind_copy(LAST - 1).wait_recv()
+            add_behind(LAST - 1, slice(None))
+
+        @pl.when(last_turn & late)
+        def _():
+            sib_last_copy(0).wait_recv()
+            sib_last_copy(1).wait_recv()
+            add_behind(LAST, slice(None))
+
+        m = k - 1 + lead
+        pl.when((m >= 0) & (m < HOPS))(lambda: process(m, k - 2))
+        pl.when(held)(lambda: receive_ahead(k))
         pl.when(k >= DRAIN)(lambda: drain(k - DRAIN))
         return 0
 
+    pl.when(lead == 1)(lambda: receive_ahead(0))
     lax.fori_loop(0, HOPS + 1, step, 0)
 
-    @pl.when(has_behind(LAST))
+    halves = has_behind(LAST) & jnp.logical_not(late)
+
+    @pl.when(halves)
     def _():
         receive_last(1)
         sib_last_copy(0).wait_recv()
@@ -330,12 +392,12 @@
     def _():
         slots_of_group(REACH)
 
-    @pl.when(has_behind(LAST))
+    @pl.when(halves)
     def _():
         sib_last_copy(1).wait_recv()
         add_behind(LAST, rows_of(1), final=True)
 
-    pl.when(jnp.logical_not(has_behind(LAST)))(lambda: write_profiles(acc[...]))
+    pl.when(jnp.logical_not(halves))(lambda: write_profiles(acc[...]))
 
     for m in range(HOPS + 1 - DRAIN, HOPS):
         drain(m)
@@ -390,8 +452,7 @@
             pltpu.VMEM((2 * BS, 2 * BS), jnp.bfloat16),
             pltpu.VMEM((BLK_DEV * BLK_DEV, BS, BS), jnp.float32),
             chunks, chunks, chunks, chunks, blocks,
-            pltpu.VMEM((1, 128), jnp.float32),
-            pltpu.VMEM((REACH, 1, 128), jnp.float32),
+            pltpu.VMEM((REACH + 1, 1, 128), jnp.float32),
             pltpu.SMEM((2, SLOTS), jnp.int32),
             pltpu.SMEM((2, windows.shape[0]), jnp.int32),
             many, many, more, more,
@@ -399,6 +460,7 @@
             few, few,
             pltpu.SemaphoreType.DMA((REACH,)), pltpu.SemaphoreType.DMA((REACH,)),
             few, pltpu.SemaphoreType.DMA((2,)),
+            pltpu.SemaphoreType.REGULAR, pltpu.SemaphoreType.REGULAR, pltpu.SemaphoreType.REGULAR,
         ],
         compiler_params=pltpu.CompilerParams(
             collective_id=0, has_side_effects=True, vmem_limit_bytes=40 << 20

time: 50.7 us -> 50 us (0.986)
  Pallas kernels: 49.9 us -> 49.3 us
    pallas_call x1, Pallas kernels: 47.6 us -> 47 us  [body(): pl.pallas_call(functools.partial(kernel, length), out_shape=(jax.ShapeDty...]
where the time goes in v4:
time: 50 us; the launch traced here: 49.9 us
  Pallas kernels  49.3 us (99%)
  between operations  0.64 us (1%)
    pallas_call x1, Pallas kernels, body(): pl.pallas_call(functools.partial(kernel, length), out_shape=(jax.ShapeDty...  47 us
    pallas_call x1, Pallas kernels, body(): pl.pallas_call(write_out, out_shape=(jax.ShapeDtypeStruct(corr.shape, cor...  2.33 us

profile of v4, /device:TPU:25, one launch (start us, length us, event | category | flops | bytes accessed | tf_op | source)
XLA Modules:
  0.0 49.9 jit_solution(17565396864164745297)
XLA Ops:
  0.6 47.0 %shard_map.50 = (f32[16,256,256]{2,1,0:T(8,128)S(1)}, bf16[4,256,256]{2,1,0:T(8,128)(2,1)S(1)}) custom-call(bf16[1024,256]{1,0:T(8,128)(2,1)} %spectra.1, s32[2,32]{1,0:T(2,128)} %bitcast.3, s32[2,512]{1,0:T(2,128)} %bitcast.2), custom_call_target="tpu_custom_call" | custom-call | tf_op jit(solution)/shard_map/pallas_call | solution.py:440
  47.6 2.3 %shard_map.51 = (f32[16,256,256]{2,1,0:T(8,128)}, bf16[1024,256]{1,0:T(8,128)(2,1)}) custom-call(f32[16,256,256]{2,1,0:T(8,128)S(1)} %get-tuple-element.4.corr, bf16[4,256,256]{2,1,0:T(8,128)(2,1)S(1)} %get-tuple-element.5.profiles), custom_call_target="tpu_custom_call" | custom-call | tf_op jit(solution)/shard_map/pallas_call | solution.py:469

commit v5 on v4

--- a/solution.py
+++ b/solution.py
@@ -47,11 +47,17 @@
     own_w[...] = total * (1.0 / SAMPLES)
 
 
+def weight(table, g, a, c, there=True):
+    lane = lax.broadcasted_iota(jnp.int32, (1, 128), 1)
+    picked = (lane == (g * BLK_DEV + a) * BLK_DEV + c) & there
+    return jnp.max(jnp.where(picked, table[...], 0.0), axis=1, keepdims=True)
+
+
 def kernel(
     length,
     spectra, pairs_in, windows_in,
-    corr, profiles,
-    own, acc, z, both, stash, ahead, behind, sib_ahead, sib_behind, sib_own, tables_w, pairs, windows,
+    corr, acc, z, last, last_w,
+    own, both, stash, ahead, behind, sib_ahead, sib_behind, sib_own, tables_w, pairs, windows,
     send_a, recv_a, send_b, recv_b,
     send_sa, recv_sa, send_sb, recv_sb, send_so, recv_so, send_w, recv_w, load_sem, table_sem, left_in, right_in, sib_in,
 ):
@@ -193,11 +199,6 @@
     def rows_at(a):
         return slice(a * BS, (a + 1) * BS)
 
-    def weight(table, g, a, c, there=True):
-        lane = lax.broadcasted_iota(jnp.int32, (1, 128), 1)
-        picked = (lane == (g * BLK_DEV + a) * BLK_DEV + c) & there
-        return jnp.max(jnp.where(picked, table[...], 0.0), axis=1, keepdims=True)
-
     def own_block(b, _):
         load(b).wait()
         sib_own_copy(b).wait_recv()
@@ -288,7 +289,13 @@
 
         @pl.when(there_b)
         def _():
-            sib_behind_copy(n).wait_recv()
+            pl.when(n < LAST)(lambda: sib_behind_copy(n).wait_recv())
+
+            @pl.when(n == LAST)
+            def _():
+                sib_last_copy(0).wait_recv()
+                sib_last_copy(1).wait_recv()
+
             both[BS:, :] = standardize(behind[n], sib_behind[n])
 
         @pl.when(jnp.logical_not(there_b))
@@ -309,22 +316,14 @@
         def _():
             slots_of_group(g)
 
-    def write_profiles(total):
-        for a in range(BLK_DEV):
-            profiles[a] = total[rows_at(a), :].astype(jnp.bfloat16)
-
-    def add_behind(m, rows, final=False):
+    def add_behind(m, rows):
         block = standardize(behind[m, rows, :], sib_behind[m, rows, :])
         grams = gram(z[...], block)
         tiles = []
         for a in range(BLK_DEV):
             w = weight(tables_w.at[REACH], REACH, m % BLK_DEV, a)
             tiles.append((grams[rows_at(a), :] * w).astype(jnp.bfloat16))
-        total = acc[...] + dot(jnp.concatenate(tiles, axis=0), block[:, :BS])
-        if final:
-            write_profiles(total)
-        else:
-            acc[...] = total
+        acc[...] += dot(jnp.concatenate(tiles, axis=0), block[:, :BS])
 
     def drain(m):
         mine = m < BLK_DEV
@@ -352,8 +351,7 @@
             receive_last(0)
             receive_last(1)
 
-        held = late & (k == LAST)
-        pl.when((k + lead < HOPS) & jnp.logical_not(held))(lambda: receive_ahead(k + lead))
+        pl.when(k + lead < HOPS)(lambda: receive_ahead(k + lead))
         lag = jnp.where(early, 1, 0)
         now = (k >= lag) & (k < LAST + lag) & jnp.logical_not(late)
         pl.when(now)(lambda: receive_behind(k - lag))
@@ -365,15 +363,8 @@
             sib_behind_copy(LAST - 1).wait_recv()
             add_behind(LAST - 1, slice(None))
 
-        @pl.when(last_turn & late)
-        def _():
-            sib_last_copy(0).wait_recv()
-            sib_last_copy(1).wait_recv()
-            add_behind(LAST, slice(None))
-
         m = k - 1 + lead
-        pl.when((m >= 0) & (m < HOPS))(lambda: process(m, k - 2))
-        pl.when(held)(lambda: receive_ahead(k))
+        pl.when((m >= 0) & (m < HOPS))(lambda: process(m, jnp.where(late, k - 1, k - 2)))
         pl.when(k >= DRAIN)(lambda: drain(k - DRAIN))
         return 0
 
@@ -382,22 +373,23 @@
 
     halves = has_behind(LAST) & jnp.logical_not(late)
 
+    pl.when(halves)(lambda: receive_last(1))
+
+    @pl.when(core == REACH // 2)
+    def _():
+        slots_of_group(REACH)
+
     @pl.when(halves)
     def _():
-        receive_last(1)
         sib_last_copy(0).wait_recv()
-        add_behind(LAST, rows_of(0))
-
-    @pl.when(core == REACH // 2)
-    def _():
-        slots_of_group(REACH)
-
-    @pl.when(halves)
-    def _():
         sib_last_copy(1).wait_recv()
-        add_behind(LAST, rows_of(1), final=True)
-
-    pl.when(jnp.logical_not(halves))(lambda: write_profiles(acc[...]))
+        last[...] = standardize(behind[LAST], sib_behind[LAST])
+        last_w[...] = tables_w[REACH]
+
+    @pl.when(jnp.logical_not(halves))
+    def _():
+        last[...] = jnp.zeros((BS, 2 * BS), jnp.bfloat16)
+        last_w[...] = jnp.zeros((1, 128), jnp.float32)
 
     for m in range(HOPS + 1 - DRAIN, HOPS):
         drain(m)
@@ -411,19 +403,27 @@
         pl.when(has_behind(LAST))(lambda part=part: sib_last_copy(part).wait_send())
 
 
-def write_out(corr, profiles, corr_out, profiles_out, sems):
-    copies = [
+def write_out(corr, acc, z, last, last_w, corr_out, profiles_out, profiles, sems):
+    tiles_out = [
         pltpu.make_async_copy(corr.at[p], corr_out.at[p], sems.at[p]) for p in range(SLOTS // 2)
     ]
-    copies += [
+    rows_out = [
         pltpu.make_async_copy(
             profiles.at[b], profiles_out.at[pl.ds(b * BS, BS), :], sems.at[SLOTS // 2 + b]
         )
         for b in range(BLK_DEV)
     ]
-    for copy in copies:
+    for copy in tiles_out:
         copy.start()
-    for copy in copies:
+    grams = lax.dot_general(z[...], last[...], NT, preferred_element_type=jnp.float32)
+    for a in range(BLK_DEV):
+        rows = slice(a * BS, (a + 1) * BS)
+        w = weight(last_w, REACH, BLK_DEV - 1, a)
+        tile = (grams[rows, :] * w).astype(jnp.bfloat16)
+        term = jnp.dot(tile, last[:, :BS], preferred_element_type=jnp.float32)
+        profiles[a] = (acc[rows, :] + term).astype(jnp.bfloat16)
+        rows_out[a].start()
+    for copy in tiles_out + rows_out:
         copy.wait()
 
 
@@ -437,18 +437,19 @@
     many = pltpu.SemaphoreType.DMA((HOPS,))
     more = pltpu.SemaphoreType.DMA((HOPS + 1,))
     few = pltpu.SemaphoreType.DMA((BLK_DEV,))
-    corr, profiles = pl.pallas_call(
+    results = pl.pallas_call(
         functools.partial(kernel, length),
         out_shape=(
             jax.ShapeDtypeStruct((SLOTS // 2, BS, BS), jnp.float32),
-            jax.ShapeDtypeStruct((BLK_DEV, BS, BS), jnp.bfloat16),
+            jax.ShapeDtypeStruct((rows, width), jnp.float32),
+            jax.ShapeDtypeStruct((rows, 2 * width), jnp.bfloat16),
+            jax.ShapeDtypeStruct((BS, 2 * width), jnp.bfloat16),
+            jax.ShapeDtypeStruct((1, 128), jnp.float32),
         ),
         in_specs=[hbm, hbm, hbm],
-        out_specs=(vmem, vmem),
+        out_specs=(vmem,) * 5,
         scratch_shapes=[
             blocks,
-            pltpu.VMEM((BLK_DEV * BS, BS), jnp.float32),
-            pltpu.VMEM((BLK_DEV * BS, 2 * BS), jnp.bfloat16),
             pltpu.VMEM((2 * BS, 2 * BS), jnp.bfloat16),
             pltpu.VMEM((BLK_DEV * BLK_DEV, BS, BS), jnp.float32),
             chunks, chunks, chunks, chunks, blocks,
@@ -469,14 +470,14 @@
     return pl.pallas_call(
         write_out,
         out_shape=(
-            jax.ShapeDtypeStruct(corr.shape, corr.dtype),
+            jax.ShapeDtypeStruct(results[0].shape, results[0].dtype),
             jax.ShapeDtypeStruct((rows, width), jnp.bfloat16),
         ),
-        in_specs=[anywhere, anywhere],
+        in_specs=[anywhere, vmem, vmem, vmem, vmem],
         out_specs=(hbm, hbm),
-        scratch_shapes=[pltpu.SemaphoreType.DMA((SLOTS // 2 + BLK_DEV,))],
-        compiler_params=pltpu.CompilerParams(vmem_limit_bytes=1 << 20),
-    )(corr, profiles)
+        scratch_shapes=[blocks, pltpu.SemaphoreType.DMA((SLOTS // 2 + BLK_DEV,))],
+        compiler_params=pltpu.CompilerParams(vmem_limit_bytes=16 << 20),
+    )(*results)
 
 
 def solution(mesh):

time: 50 us -> 49.1 us (0.982)
  Pallas kernels: 49.3 us -> 48.4 us
    pallas_call x1, Pallas kernels: 47 us -> 46 us  [body(): pl.pallas_call(functools.partial(kernel, length), out_shape=(jax.ShapeDty...]
where the time goes in v5:
time: 49.1 us; the launch traced here: 49 us
  Pallas kernels  48.4 us (99%)
  between operations  0.64 us (1%)
    pallas_call x1, Pallas kernels, body(): pl.pallas_call(functools.partial(kernel, length), out_shape=(jax.ShapeDty...  46 us
    pallas_call x1, Pallas kernels, body(): pl.pallas_call(write_out, out_shape=(jax.ShapeDtypeStruct(results[0].shap...  2.39 us

profile of v5, /device:TPU:25, one launch (start us, length us, event | category | flops | bytes accessed | tf_op | source)
XLA Modules:
  0.0 49.0 jit_solution(7642368663595311490)
XLA Ops:
  0.6 46.0 %shard_map.50 = (f32[16,256,256]{2,1,0:T(8,128)S(1)}, f32[1024,256]{1,0:T(8,128)S(1)}, bf16[1024,512]{1,0:T(8,128)(2,1)S(1)}, bf16[256,512]{1,0:T(8,128)(2,1)S(1)}, f32[1,128]{1,0:T(1,128)S(1)}) custom-call(bf16[1024,256]{1,0:T(8,128)(2,1)} %spectra.1, s32[2,32]{1,0:T(2,128)} %bitcast.3, s32[2,512]{1,0:T(2,128)} %bitcast.2), custom_call_target="tpu_custom_call" | custom-call | tf_op jit(solution)/shard_map/pallas_call | solution.py:440
  46.7 2.4 %shard_map.51 = (f32[16,256,256]{2,1,0:T(8,128)}, bf16[1024,256]{1,0:T(8,128)(2,1)}) custom-call(f32[16,256,256]{2,1,0:T(8,128)S(1)} %get-tuple-element.7.corr, f32[1024,256]{1,0:T(8,128)S(1)} %get-tuple-element.8.acc, bf16[1024,512]{1,0:T(8,128)(2,1)S(1)} %get-tuple-element.9.z, bf16[256,512]{1,0:T(8,128)(2,1)S(1)} %get-tuple-element.10.last, ...), custom_call_target="tpu_custom_call" | custom-call | tf_op jit(solution)/shard_map/pallas_call | solution.py:470

commit v6 on v5

--- a/solution.py
+++ b/solution.py
@@ -53,6 +53,17 @@
     return jnp.max(jnp.where(picked, table[...], 0.0), axis=1, keepdims=True)
 
 
+def standardize(mine, other):
+    x1, x2 = mine.astype(jnp.float32), other.astype(jnp.float32)
+    total = jnp.sum(x1 + x2, axis=1, keepdims=True)
+    squares = jnp.sum(x1 * x1 + x2 * x2, axis=1, keepdims=True)
+    mean = total / SAMPLES
+    var = squares / SAMPLES - mean * mean
+    inv = lax.rsqrt(var + 1e-05)
+    z1, z2 = (x1 - mean) * inv, (x2 - mean) * inv
+    return jnp.concatenate([z1.astype(jnp.bfloat16), z2.astype(jnp.bfloat16)], axis=1)
+
+
 def kernel(
     length,
     spectra, pairs_in, windows_in,
@@ -180,16 +191,6 @@
     pair_weights(pairs, windows, me * BLK_DEV, own_w)
     pl.when(has_right)(lambda: w_copy(0).start())
 
-    def standardize(mine, other):
-        x1, x2 = mine.astype(jnp.float32), other.astype(jnp.float32)
-        total = jnp.sum(x1 + x2, axis=1, keepdims=True)
-        squares = jnp.sum(x1 * x1 + x2 * x2, axis=1, keepdims=True)
-        mean = total / SAMPLES
-        var = squares / SAMPLES - mean * mean
-        inv = lax.rsqrt(var + 1e-05)
-        z1, z2 = (x1 - mean) * inv, (x2 - mean) * inv
-        return jnp.concatenate([z1.astype(jnp.bfloat16), z2.astype(jnp.bfloat16)], axis=1)
-
     def gram(za, zc):
         return lax.dot_general(za, zc, NT, preferred_element_type=jnp.float32)
 
@@ -358,11 +359,6 @@
         last_turn = (k == HOPS) & has_behind(LAST)
         pl.when(last_turn & jnp.logical_not(late))(lambda: receive_last(0))
 
-        @pl.when(last_turn & (lead == 1))
-        def _():
-            sib_behind_copy(LAST - 1).wait_recv()
-            add_behind(LAST - 1, slice(None))
-
         m = k - 1 + lead
         pl.when((m >= 0) & (m < HOPS))(lambda: process(m, jnp.where(late, k - 1, k - 2)))
         pl.when(k >= DRAIN)(lambda: drain(k - DRAIN))
@@ -373,17 +369,23 @@
 
     halves = has_behind(LAST) & jnp.logical_not(late)
 
+    @pl.when(core == REACH // 2)
+    def _():
+        slots_of_group(REACH)
+
     pl.when(halves)(lambda: receive_last(1))
 
-    @pl.when(core == REACH // 2)
-    def _():
-        slots_of_group(REACH)
+    @pl.when(halves & (lead == 1))
+    def _():
+        sib_behind_copy(LAST - 1).wait_recv()
+        add_behind(LAST - 1, slice(None))
 
     @pl.when(halves)
     def _():
         sib_last_copy(0).wait_recv()
         sib_last_copy(1).wait_recv()
-        last[...] = standardize(behind[LAST], sib_behind[LAST])
+        last[:, :BS] = behind[LAST]
+        last[:, BS:] = sib_behind[LAST]
         last_w[...] = tables_w[REACH]
 
     @pl.when(jnp.logical_not(halves))
@@ -415,12 +417,13 @@
     ]
     for copy in tiles_out:
         copy.start()
-    grams = lax.dot_general(z[...], last[...], NT, preferred_element_type=jnp.float32)
+    block = standardize(last[:, :BS], last[:, BS:])
+    grams = lax.dot_general(z[...], block, NT, preferred_element_type=jnp.float32)
     for a in range(BLK_DEV):
         rows = slice(a * BS, (a + 1) * BS)
         w = weight(last_w, REACH, BLK_DEV - 1, a)
         tile = (grams[rows, :] * w).astype(jnp.bfloat16)
-        term = jnp.dot(tile, last[:, :BS], preferred_element_type=jnp.float32)
+        term = jnp.dot(tile, block[:, :BS], preferred_element_type=jnp.float32)
         profiles[a] = (acc[rows, :] + term).astype(jnp.bfloat16)
         rows_out[a].start()
     for copy in tiles_out + rows_out:

time: 49.1 us -> 48.7 us (level)
  Pallas kernels: 48.4 us -> 47.9 us
where the time goes in v6:
time: 48.7 us; the launch traced here: 48.6 us
  Pallas kernels  47.9 us (98%)
  between operations  0.64 us (1%)
    pallas_call x1, Pallas kernels, body(): pl.pallas_call(functools.partial(kernel, length), out_shape=(jax.ShapeDty...  45.5 us
    pallas_call x1, Pallas kernels, body(): pl.pallas_call(write_out, out_shape=(jax.ShapeDtypeStruct(results[0].shap...  2.4 us

profile of v6, /device:TPU:25, one launch (start us, length us, event | category | flops | bytes accessed | tf_op | source)
XLA Modules:
  0.0 48.6 jit_solution(4992123226300327009)
XLA Ops:
  0.6 45.5 %shard_map.50 = (f32[16,256,256]{2,1,0:T(8,128)S(1)}, f32[1024,256]{1,0:T(8,128)S(1)}, bf16[1024,512]{1,0:T(8,128)(2,1)S(1)}, bf16[256,512]{1,0:T(8,128)(2,1)S(1)}, f32[1,128]{1,0:T(1,128)S(1)}) custom-call(bf16[1024,256]{1,0:T(8,128)(2,1)} %spectra.1, s32[2,32]{1,0:T(2,128)} %bitcast.3, s32[2,512]{1,0:T(2,128)} %bitcast.2), custom_call_target="tpu_custom_call" | custom-call | tf_op jit(solution)/shard_map/pallas_call | solution.py:443
  46.2 2.4 %shard_map.51 = (f32[16,256,256]{2,1,0:T(8,128)}, bf16[1024,256]{1,0:T(8,128)(2,1)}) custom-call(f32[16,256,256]{2,1,0:T(8,128)S(1)} %get-tuple-element.7.corr, f32[1024,256]{1,0:T(8,128)S(1)} %get-tuple-element.8.acc, bf16[1024,512]{1,0:T(8,128)(2,1)S(1)} %get-tuple-element.9.z, bf16[256,512]{1,0:T(8,128)(2,1)S(1)} %get-tuple-element.10.last, ...), custom_call_target="tpu_custom_call" | custom-call | tf_op jit(solution)/shard_map/pallas_call | solution.py:473

commit v7 on v6

--- a/solution.py
+++ b/solution.py
@@ -16,7 +16,7 @@
 LAST = HOPS - 1
 HALF = BS // 2
 COLUMN = 8
-DRAIN = 5
+DRAIN = 4
 SAMPLES = 512
 MESH = pl.DeviceIdType.MESH
 NT = (((1,), (1,)), ((), ()))

time: 48.7 us -> 48.6 us (level)
  no operation moved by 1% of the time
where the time goes in v7:
time: 48.6 us
  Pallas kernels  47.9 us (99%)
  between operations  0.64 us (1%)
    pallas_call x1, Pallas kernels, body(): pl.pallas_call(functools.partial(kernel, length), out_shape=(jax.ShapeDty...  45.5 us
    pallas_call x1, Pallas kernels, body(): pl.pallas_call(write_out, out_shape=(jax.ShapeDtypeStruct(results[0].shap...  2.4 us

profile of v7, /device:TPU:25, one launch (start us, length us, event | category | flops | bytes accessed | tf_op | source)
XLA Modules:
  0.0 48.6 jit_solution(5164309602362981051)
XLA Ops:
  0.6 45.5 %shard_map.50 = (f32[16,256,256]{2,1,0:T(8,128)S(1)}, f32[1024,256]{1,0:T(8,128)S(1)}, bf16[1024,512]{1,0:T(8,128)(2,1)S(1)}, bf16[256,512]{1,0:T(8,128)(2,1)S(1)}, f32[1,128]{1,0:T(1,128)S(1)}) custom-call(bf16[1024,256]{1,0:T(8,128)(2,1)} %spectra.1, s32[2,32]{1,0:T(2,128)} %bitcast.3, s32[2,512]{1,0:T(2,128)} %bitcast.2), custom_call_target="tpu_custom_call" | custom-call | tf_op jit(solution)/shard_map/pallas_call | solution.py:443
  46.2 2.4 %shard_map.51 = (f32[16,256,256]{2,1,0:T(8,128)}, bf16[1024,256]{1,0:T(8,128)(2,1)}) custom-call(f32[16,256,256]{2,1,0:T(8,128)S(1)} %get-tuple-element.7.corr, f32[1024,256]{1,0:T(8,128)S(1)} %get-tuple-element.8.acc, bf16[1024,512]{1,0:T(8,128)(2,1)S(1)} %get-tuple-element.9.z, bf16[256,512]{1,0:T(8,128)(2,1)S(1)} %get-tuple-element.10.last, ...), custom_call_target="tpu_custom_call" | custom-call | tf_op jit(solution)/shard_map/pallas_call | solution.py:473
